TPU v7x, 256 devices: a whole 4x4x8 slice. The times are simulated.
256 devices in a mesh: ctx: 16 (over z, core), exp: 16 (over x, y).
Axes of the slice: x: 4, y: 4, z: 8, core: 2. Of those that a mesh axis runs over, the one named last changes fastest.
Arguments:
- inner_input: bfloat16 [8192, 8192], P('ctx', 'exp'), may hold values from -6 to 6
- gate_input: bfloat16 [8192, 8192], P('ctx', 'exp'), may hold values from -6 to 6
- coupling_input: bfloat16 [8192, 256], P('ctx'), may hold values from -6 to 6
- step_input: float32 [8192, 128], P('ctx', 'exp'), may hold values from -7 to 140
- conv_inner: float32 [4, 8192], P(None, 'exp'), may hold values from -3 to 3
- conv_coupling: float32 [4, 256], replicated, may hold values from -3 to 3
- decay_log: float32 [128], P('exp'), may hold values from -5.3 to -2.5
- skip_gain: float32 [128], P('exp'), may hold values from 0.5 to 2
- norm_gain: float32 [8192], P('exp'), may hold values from 0.1 to 1.9
- out_weight: bfloat16 [8192, 4096], P('exp'), may hold values from -0.0625 to 0.0625
- residual: bfloat16 [8192, 4096], P(('ctx', 'exp')), may hold values from -6 to 6
- moe_gain: float32 [4096], replicated, may hold values from 0.1 to 1.9
- router_weight: bfloat16 [4096, 72], replicated, may hold values from -0.1875 to 0.1875
- routes: int32 [8192, 10], P(('ctx', 'exp')), may hold values from 0 to 71, all different within a row
- priority: int32 [256, 32], P(('ctx', 'exp')), may hold values from 0 to 31, each once within a row
- expert_in: bfloat16 [16, 4096, 1536], P('exp', 'ctx'), may hold values from -0.09375 to 0.09375
- expert_out: bfloat16 [16, 4096, 768], P('exp', 'ctx'), may hold values from -0.21875 to 0.21875
Outputs:
- hidden: float32 [8192, 4096], P(('ctx', 'exp'))
- moe_out: float32 [8192, 4096], P(('ctx', 'exp'))
Inputs may be any that keep to these rules, and one draw needn't show every extreme that they name: `routes`: each token names 10 different experts. `priority`: the 32 tokens of each row carry distinct priorities.
All inputs are finite; a program needn't handle non-finite values.
Results may differ from a plain program's by a relative error of at most 0.029.
Values may be sent and summed in bfloat16 or wider, within the bound.
A program may use at most 128 MiB of HBM per device.

v0:
```python
import jax
import jax.numpy as jnp
from jax import lax
from jax.sharding import PartitionSpec as P

HDIM = 64
STATE = 128
KCONV = 4
NEXP = 72
TOPK = 10
FFE = 768
SPAN = 256
INNER = 8192


EPS = 1e-05
HIGH = lax.Precision.HIGHEST


def shifted(array, axis, by):
    devices = lax.axis_size(axis)
    pairs = [(i, i + by) for i in range(devices) if 0 <= i + by < devices]
    return lax.ppermute(array, axis, pairs)


def carried_in(part, axis, combine, identity):
    place = lax.axis_index(axis)
    gathered = jax.tree.map(lambda a: lax.all_gather(a, axis), part)
    state = jax.tree.map(lambda a, e: jnp.zeros_like(a) + jnp.asarray(e, a.dtype), part, identity)

    def one(step, state):
        return combine(
            state, jax.tree.map(lambda a: lax.dynamic_index_in_dim(a, step, 0, False), gathered)
        )

    return lax.fori_loop(0, place, one, state)


def causal_conv(values, before, weight):
    count = values.shape[0]
    padded = jnp.concatenate([before.astype(jnp.float32), values.astype(jnp.float32)], axis=0)
    total = jnp.zeros((count, values.shape[1]), jnp.float32)
    for k in range(KCONV):
        total = total + weight[k][None, :] * padded[k : k + count]
    return jax.nn.silu(total).astype(jnp.bfloat16)


def join_states(earlier, later):
    return (earlier[0] * later[0], later[0][:, None, None] * earlier[1] + later[1])


def body(
    inner_input,
    gate_input,
    coupling_input,
    step_input,
    conv_inner,
    conv_coupling,
    decay_log,
    skip_gain,
    norm_gain,
    out_weight,
    residual,
    moe_gain,
    router_weight,
    routes,
    priority,
    expert_in,
    expert_out,
):
    width = inner_input.shape[1]
    heads = decay_log.shape[0]
    count = inner_input.shape[0]
    blocks = count // SPAN
    edges = jnp.concatenate(
        [inner_input[count - (KCONV - 1) :], coupling_input[count - (KCONV - 1) :]], axis=1
    )
    before = shifted(edges, "ctx", 1)
    inner = causal_conv(inner_input, before[:, :width], conv_inner)
    coupling = causal_conv(coupling_input, before[:, width:], conv_coupling)
    steps = jax.nn.softplus(step_input).reshape(blocks, SPAN, heads)
    inner_parts = inner.reshape(blocks, SPAN, heads, HDIM)
    input_parts = coupling[:, :STATE].reshape(blocks, SPAN, STATE)
    output_parts = coupling[:, STATE:].reshape(blocks, SPAN, STATE)
    rate = steps * (-jnp.exp(decay_log))[None, None, :]
    cums = jnp.cumsum(rate, axis=1)
    scores = jnp.einsum(
        "cin,cjn->cij", output_parts, input_parts, preferred_element_type=jnp.float32
    )
    above = (jnp.arange(SPAN)[:, None] >= jnp.arange(SPAN)[None, :])[None, None]
    flipped = jnp.swapaxes(cums, 1, 2)
    spread = flipped[:, :, :, None] - flipped[:, :, None, :]
    decay = jnp.where(above, jnp.exp(jnp.where(above, spread, 0.0)), 0.0)
    mixing = (scores[:, None] * decay * jnp.swapaxes(steps, 1, 2)[:, :, None, :]).astype(
        jnp.bfloat16
    )
    local = jnp.einsum("chij,cjhp->cihp", mixing, inner_parts, preferred_element_type=jnp.float32)
    inner_wide = inner_parts.astype(jnp.float32)
    tail = jnp.exp(cums[:, -1:, :] - cums) * steps
    states = jnp.einsum(
        "cjh,cjn,cjhp->chnp", tail, input_parts.astype(jnp.float32), inner_wide, precision=HIGH
    )
    drops = jnp.exp(cums[:, -1, :])
    running = jnp.zeros((heads, STATE, HDIM), jnp.float32)
    reach = jnp.ones((heads,), jnp.float32)
    starts = []
    reaches = []
    for k in range(blocks):
        starts.append(running)
        reaches.append(reach)
        running = drops[k][:, None, None] * running + states[k]
        reach = reach * drops[k]
    neutral = (jnp.ones((heads,), jnp.float32), jnp.zeros((heads, STATE, HDIM), jnp.float32))
    incoming = carried_in((reach, running), "ctx", join_states, neutral)[1]
    entry = jnp.stack([reaches[k][:, None, None] * incoming + starts[k] for k in range(blocks)])
    carried = jnp.einsum(
        "cin,cih,chnp->cihp", output_parts.astype(jnp.float32), jnp.exp(cums), entry, precision=HIGH
    )
    mixed = (local + carried + skip_gain[None, None, :, None] * inner_wide).reshape(count, width)
    gated = mixed * jax.nn.silu(gate_input.astype(jnp.float32))
    squares = jnp.sum(gated * gated, axis=1)
    scaled = (gated * norm_gain[None, :]).astype(jnp.bfloat16)
    projected = jnp.dot(scaled, out_weight, preferred_element_type=jnp.float32)
    owned = lax.psum_scatter(
        projected.astype(jnp.bfloat16), "exp", scatter_dimension=0, tiled=True
    ).astype(jnp.float32)
    owned_squares = lax.psum_scatter(squares, "exp", scatter_dimension=0, tiled=True)
    mamba_out = owned * lax.rsqrt(owned_squares / INNER + EPS)[:, None]
    hidden = residual.astype(jnp.float32) + mamba_out
    tokens = hidden.shape[0]
    flight = lax.axis_size("exp")
    capacity = max(2, 2 * tokens * TOPK // NEXP)
    normed = (
        hidden * lax.rsqrt(jnp.mean(hidden * hidden, axis=1) + EPS)[:, None] * moe_gain[None, :]
    ).astype(jnp.bfloat16)
    logits = jnp.dot(normed, router_weight, preferred_element_type=jnp.float32)
    table = routes[:, :, None] == jnp.arange(NEXP, dtype=jnp.int32)[None, None, :]
    picked = jnp.sum(jnp.where(table, logits[:, None, :], 0.0), axis=2)
    raised = jnp.exp(picked)
    probs = raised / jnp.sum(raised, axis=1, keepdims=True)
    match = routes[:, :, None] == jnp.arange(flight, dtype=jnp.int32)[None, None, :]
    member = jnp.sum(match.astype(jnp.int32), axis=1)
    share = jnp.sum(jnp.where(match, probs[:, :, None], 0.0), axis=1).astype(jnp.bfloat16)
    order = priority[0]
    earlier = (order[None, :] < order[:, None]).astype(jnp.int32)
    rank = jnp.sum(earlier[:, :, None] * member[None, :, :], axis=1)
    kept = (member > 0) & (rank < capacity)
    slots = kept[:, :, None] & (
        rank[:, :, None] == jnp.arange(capacity, dtype=jnp.int32)[None, None, :]
    )
    select = jnp.transpose(slots, (1, 2, 0)).astype(jnp.bfloat16)
    outbound = jnp.einsum("fst,td->fsd", select, normed, preferred_element_type=jnp.float32).astype(
        jnp.bfloat16
    )
    arrived = lax.all_to_all(outbound, "exp", split_axis=0, concat_axis=0, tiled=True)
    rows = arrived.reshape(flight * capacity, normed.shape[1])
    slices = lax.axis_size("ctx")
    whole_in = lax.all_gather(expert_in[0], "ctx", axis=0, tiled=True)
    slice_width = rows.shape[1] // slices
    parts = jnp.einsum(
        "rkw,kwf->krf",
        rows.reshape(rows.shape[0], slices, slice_width),
        whole_in.reshape(slices, slice_width, 2 * FFE),
        preferred_element_type=jnp.float32,
    ).astype(jnp.bfloat16)
    units = jnp.sum(lax.optimization_barrier(parts).astype(jnp.float32), axis=0)
    activated = (jax.nn.silu(units[:, :FFE]) * units[:, FFE:]).astype(jnp.bfloat16)
    answer = jnp.einsum(
        "rf,df->rd",
        activated,
        lax.all_gather(expert_out[0], "ctx", axis=0, tiled=True),
        preferred_element_type=jnp.float32,
    ).astype(jnp.bfloat16)
    returned = lax.all_to_all(
        answer.reshape(flight, capacity, answer.shape[1]),
        "exp",
        split_axis=0,
        concat_axis=0,
        tiled=True,
    )
    weights = select * jnp.transpose(share)[:, None, :]
    moe_out = jnp.einsum("fst,fsd->td", weights, returned, preferred_element_type=jnp.float32)
    return (hidden, moe_out)


def solution(mesh):
    placed = (
        P("ctx", "exp"),
        P("ctx", "exp"),
        P("ctx", None),
        P("ctx", "exp"),
        P(None, "exp"),
        P(),
        P("exp"),
        P("exp"),
        P("exp"),
        P("exp", None),
        P(("ctx", "exp"), None),
        P(),
        P(),
        P(("ctx", "exp"), None),
        P(("ctx", "exp"), None),
        P("exp", "ctx", None),
        P("exp", "ctx", None),
    )
    return jax.shard_map(
        body,
        mesh=mesh,
        in_specs=placed,
        out_specs=(P(("ctx", "exp"), None), P(("ctx", "exp"), None)),
        check_vma=False,
    )
```

profile of v0, /device:TPU:1, one launch (start us, length us, event | category | flops | bytes accessed | tf_op | source)
XLA Modules:
  0.0 353.6 jit_solution(14720117451480724429)
XLA Ops:
  9.5 4.9 %collective-permute-start = (bf16[3,768]{0,1:T(8,128)(2,1)}, bf16[3,768]{0,1:T(8,128)(2,1)S(1)}, u32[]{:S(2)}, u32[]{:S(2)}) collective-permute-start(bf16[3,768]{0,1:T(8,128)(2,1)} %copy.91), channel_id=1, source_target_pairs={{0,16},{16,32},{32,48},{48,64},{64,80},{80,96},{96,112},{112,128},... | collective-permute-start | bytes 13832 | tf_op jit(solution)/shard_map/ppermute | solution.py:23
  15.9 1.1 reduce-window.6
  20.5 1.0 convert_element_type.80
  21.5 1.3 copy.92
  23.4 1.5 multiply_convert_fusion.9
  26.8 18.8 %all-gather.2 = f32[16,1,8]{2,1,0:T(1,128)} all-gather(f32[1,1,8]{2,1,0:T(1,128)S(1)} %get-tuple-element.98), channel_id=1, replica_groups=mesh['ctx'=16,'exp'=16] {'ctx'}, dimensions={0}, use_global_device_ids=true | all-gather | bytes 544 | tf_op jit(solution)/shard_map/all_gather | solution.py:28
  46.3 1.0 fusion.67
  47.3 23.2 %all-gather.7.cloned.1.call-done = f32[16,8,128,64]{2,3,1,0:T(8,128)} async-done(((f32[1,8,128,64]{2,3,1,0:T(8,128)}), f32[16,8,128,64]{2,3,1,0:T(8,128)}) %all-gather.7.cloned.1.call-update) | async-done | bytes 4194320 | tf_op jit(solution)/shard_map/all_gather | solution.py:28
  70.6 2.1 while.12
  73.6 1.5 fusion.68
  75.2 2.3 fusion.17
  78.4 1.3 copy-done.10
  79.7 4.6 %convolution_convert_fusion = bf16[512,4096]{1,0:T(8,128)(2,1)} fusion(bf16[512,4096]{1,0:T(8,128)(2,1)S(1)} %copy-done.10, f32[512]{0:T(512)S(1)} %copy-done.11, f32[512,512]{0,1:T(8,128)S(1)} %bitcast.109, bf16[512,512]{0,1:T(8,128)(2,1)S(1)} %copy.102), kind=kOutput, calls=%fused_computation.6 | convolution fusion | flops 2151677952 | bytes 9963520 | tf_op jit(solution)/shard_map/dot_general | solution.py:123
  88.2 32.9 %all-reduce = f32[512]{0:T(512)S(1)} all-reduce(f32[512]{0:T(512)S(1)} %multiply_reduce_fusion), channel_id=5, replica_groups=mesh['ctx'=16,'exp'=16] {'exp'}, use_global_device_ids=true, to_apply=%region_6.7.clone | all-reduce | flops 512 | bytes 4096
  121.1 70.9 %reduce-scatter.2.cloned.1.call-done = bf16[32,4096]{1,0:T(8,128)(2,1)} async-done(((bf16[512,4096]{1,0:T(8,128)(2,1)}), bf16[32,4096]{1,0:T(8,128)(2,1)}) %reduce-scatter.2.cloned.1.call-update) | async-done | bytes 262160 | tf_op jit(solution)/shard_map/reduce_scatter | solution.py:124
  192.1 1.2 multiply_reduce_fusion.1
  193.8 17.5 %all_to_all.10 = bf16[16,8,4096]{2,1,0:T(8,128)(2,1)S(1)} all-to-all(bf16[16,8,4096]{2,1,0:T(8,128)(2,1)S(1)} %convolution_convert_fusion.2), channel_id=1, replica_groups=mesh['ctx'=16,'exp'=16] {'exp'}, dimensions={0} | all-to-all | bytes 2097152 | tf_op jit(solution)/shard_map/all_to_all | solution.py:155
  211.6 59.4 %all-gather.9.cloned.1.call-done = bf16[1,4096,1536]{2,1,0:T(8,128)(2,1)} async-done(((bf16[1,256,1536]{2,1,0:T(8,128)(2,1)}), bf16[1,4096,1536]{2,1,0:T(8,128)(2,1)}) %all-gather.9.cloned.1.call-update) | async-done | bytes 12582928 | tf_op jit(solution)/shard_map/all_gather | solution.py:158
  271.0 6.6 %convolution_convert_fusion.1 = bf16[16,128,1536]{2,1,0:T(8,128)(2,1)S(1)} fusion(bf16[16,256,1536]{2,1,0:T(8,128)(2,1)} %bitcast.107, bf16[128,16,256]{2,1,0:T(8,128)(2,1)S(1)} %bitcast.108), kind=kOutput, calls=%fused_computation.7 | convolution fusion | flops 1613758464 | bytes 19922944 | tf_op jit(solution)/shard_map/rkw,kwf->krf/dot_general | solution.py:160
  278.5 38.8 %all-gather.11.cloned.1.call-done = bf16[1,4096,768]{2,1,0:T(8,128)(2,1)} async-done(((bf16[1,256,768]{2,1,0:T(8,128)(2,1)}), bf16[1,4096,768]{2,1,0:T(8,128)(2,1)}) %all-gather.11.cloned.1.call-update) | async-done | bytes 6291472 | tf_op jit(solution)/shard_map/all_gather | solution.py:171
  317.3 5.9 %fusion.5 = bf16[16,8,4096]{2,1,0:T(8,128)(2,1)} fusion(bf16[1,4096,768]{2,1,0:T(8,128)(2,1)} %all-gather.11.cloned.1.call-done, f32[128,1536]{1,0:T(8,128)S(1)} %convert_reduce_fusion), kind=kOutput, calls=%fused_computation.10 | convolution fusion | flops 806420480 | bytes 8126464 | tf_op jit(solution)/shard_map/rf,df->rd/dot_general | solution.py:168
  323.2 6.5 %all-to-all-start.1 = ((bf16[16,8,4096]{2,1,0:T(8,128)(2,1)}), bf16[16,8,4096]{2,1,0:T(8,128)(2,1)S(1)}, u32[]{:S(2)}, u32[]{:S(2)}) async-start(bf16[16,8,4096]{2,1,0:T(8,128)(2,1)} %fusion.5), calls=%async_computation.2 | async-start | bytes 2097152 | tf_op jit(solution)/shard_map/all_to_all | solution.py:174
  330.3 15.2 %all-to-all-done.1 = bf16[16,8,4096]{2,1,0:T(8,128)(2,1)S(1)} async-done(((bf16[16,8,4096]{2,1,0:T(8,128)(2,1)}), bf16[16,8,4096]{2,1,0:T(8,128)(2,1)S(1)}, u32[]{:S(2)}, u32[]{:S(2)}) %all-to-all-start.1) | async-done | bytes 1048608 | tf_op jit(solution)/shard_map/all_to_all | solution.py:174
  345.5 1.5 convolution_bitcast_fusion
  (93 shorter events, 19.7 us)
Async XLA Ops:
  7.2 322.5 %copy-start = (bf16[4096,72]{0,1:T(8,128)(2,1)S(1)}, bf16[4096,72]{0,1:T(8,128)(2,1)}, u32[]{:S(2)}) copy-start(bf16[4096,72]{0,1:T(8,128)(2,1)} %param.31) | copy-start | bytes 1769476
  7.2 63.3 %all-gather.7.cloned.1.call-start = ((), (), s32[]{:S(2)}) async-start(), calls=%async_computation.3 | async-start | bytes 4456448 | tf_op jit(solution)/shard_map/all_gather | solution.py:28
  9.5 13.3 %collective-permute-start = (bf16[3,768]{0,1:T(8,128)(2,1)}, bf16[3,768]{0,1:T(8,128)(2,1)S(1)}, u32[]{:S(2)}, u32[]{:S(2)}) collective-permute-start(bf16[3,768]{0,1:T(8,128)(2,1)} %copy.91), channel_id=1, source_target_pairs={{0,16},{16,32},{32,48},{48,64},{64,80},{80,96},{96,112},{112,128},... | collective-permute-start | bytes 13832 | tf_op jit(solution)/shard_map/ppermute | solution.py:23
  20.5 5.2 %copy-start.8 = (f32[8]{0:T(128)}, f32[8]{0:T(128)S(1)}, u32[]{:S(2)}) copy-start(f32[8]{0:T(128)S(1)} %broadcast_multiply_fusion) | copy-start | bytes 100
  22.7 3.9 %copy-start.4 = (bf16[512,512]{1,0:T(8,128)(2,1)S(1)}, bf16[512,512]{1,0:T(8,128)(2,1)}, u32[]{:S(2)}) copy-start(bf16[512,512]{1,0:T(8,128)(2,1)} %param.20) | copy-start | bytes 1572868
  23.4 47.2 %copy-start.2 = (bf16[512,128]{1,0:T(8,128)(2,1)}, bf16[512,128]{1,0:T(8,128)(2,1)S(1)}, u32[]{:S(2)}) copy-start(bf16[512,128]{1,0:T(8,128)(2,1)S(1)} %get-tuple-element.87) | copy-start | bytes 393220
  26.5 165.5 %reduce-scatter.2.cloned.1.call-start = ((), (), s32[]{:S(2)}) async-start(), calls=%async_computation.4 | async-start | bytes 4456448 | tf_op jit(solution)/shard_map/reduce_scatter | solution.py:124
  72.6 2.5 copy-start.3
  77.5 2.2 copy-start.10
  77.5 2.2 copy-start.11
  84.3 1.4 copy-start.6
  84.3 1.4 copy-start.9
  84.3 2.2 copy-start.12
  84.3 107.7 %copy-start.5 = (bf16[32,4096]{1,0:T(8,128)(2,1)S(1)}, bf16[32,4096]{1,0:T(8,128)(2,1)}, u32[]{:S(2)}) copy-start(bf16[32,4096]{1,0:T(8,128)(2,1)} %param.29) | copy-start | bytes 786436
  84.3 109.0 %copy-start.7 = (f32[4096]{0:T(1024)S(1)}, f32[4096]{0:T(1024)}, u32[]{:S(2)}) copy-start(f32[4096]{0:T(1024)} %param.30) | copy-start | bytes 49156
  84.4 186.6 %all-gather.9.cloned.1.call-start = ((), (), s32[]{:S(2)}) async-start(), calls=%async_computation.5 | async-start | bytes 13369344 | tf_op jit(solution)/shard_map/all_gather | solution.py:158
  85.1 232.1 %all-gather.11.cloned.1.call-start = ((), (), s32[]{:S(2)}) async-start(), calls=%async_computation.6 | async-start | bytes 6684672 | tf_op jit(solution)/shard_map/all_gather | solution.py:171
  193.3 136.4 %copy-start.1 = (f32[32,4096]{1,0:T(8,128)}, f32[32,4096]{1,0:T(8,128)S(1)}, u32[]{:S(2)}) copy-start(f32[32,4096]{1,0:T(8,128)S(1)} %get-tuple-element.83) | copy-start | bytes 1572868
  323.2 22.3 %all-to-all-start.1 = ((bf16[16,8,4096]{2,1,0:T(8,128)(2,1)}), bf16[16,8,4096]{2,1,0:T(8,128)(2,1)S(1)}, u32[]{:S(2)}, u32[]{:S(2)}) async-start(bf16[16,8,4096]{2,1,0:T(8,128)(2,1)} %fusion.5), calls=%async_computation.2 | async-start | bytes 2097152 | tf_op jit(solution)/shard_map/all_to_all | solution.py:174
Sparse Core Ops, SparseCore 0:
  26.7 43.8 all-gather.6
  84.5 107.5 reduce-scatter.1
  193.9 77.0 all-gather.8
  272.7 44.5 all-gather.10
where the time goes:
time: 356 us; the launch traced here: 354 us
  waiting for transfers between devices  209 us (59%)
  blocking collectives  69.2 us (19%)
  matrix products  25 us (7%)
  between operations  14.8 us (4%)
  other arithmetic  13 us (4%)
  starting transfers between devices  11.6 us (3%)
  local copies, waits for them, and re-layouts  11.2 us (3%)
    reduce_scatter x1, waiting for transfers between devices, body(): lax.psum_scatter(projected.astype(jnp.bfloat16), 'exp', scatter_dimension...  70.9 us
    all_gather x1, waiting for transfers between devices, body(): whole_in = lax.all_gather(expert_in[0], 'ctx', axis=0, tiled=True)  59.4 us
    all_gather x1, waiting for transfers between devices, body(): lax.all_gather(expert_out[0], 'ctx', axis=0, tiled=True)  38.8 us
    unnamed x1, blocking collectives  32.9 us
    all_gather x1, waiting for transfers between devices, carried_in(): gathered = jax.tree.map(lambda a: lax.all_gather(a, axis), part)  23.2 us
    all_gather x1, blocking collectives, carried_in(): gathered = jax.tree.map(lambda a: lax.all_gather(a, axis), part)  18.8 us
    all_to_all x1, blocking collectives, body(): lax.all_to_all(outbound, 'exp', split_axis=0, concat_axis=0, tiled=True)  17.5 us
    all_to_all x1, waiting for transfers between devices, body(): lax.all_to_all(answer.reshape(flight, capacity, answer.shape[1]), 'exp',...  15.2 us
  transfers between devices with their start and end apart: 6, of which 5 were waited for; matrix products, arithmetic and copies ran while one was open for 6% of the time, Pallas kernels for 0%

commit v1 on v0

v1 whole, which is shorter than its diff:
```python
import jax
import jax.numpy as jnp
from jax import lax
from jax.experimental import pallas as pl
from jax.experimental.pallas import tpu as pltpu
from jax.sharding import PartitionSpec as P

HDIM = 64
STATE = 128
KCONV = 4
NEXP = 72
TOPK = 10
FFE = 768
SPAN = 256
INNER = 8192
D = 4096
HEADS = 8
WIDTH = 512
COUNT = 512
TOK = 32
CAP = 8
FLIGHT = 16
SLICE = 256
RING = 8
CHUNKS = 4

EPS = 1e-05
HIGH = lax.Precision.HIGHEST
F32 = jnp.float32
BF16 = jnp.bfloat16
MESH = pl.DeviceIdType.MESH
VMEM_LIMIT = 56 * 1024 * 1024


def vmem():
    return pl.BlockSpec(memory_space=pltpu.VMEM)


def anyspace():
    return pl.BlockSpec(memory_space=pl.ANY)


def shaped(shape, dtype):
    return jax.ShapeDtypeStruct(shape, dtype)


def silu(x):
    return x * jax.nn.sigmoid(x)


def where_am_i():
    c = lax.axis_index("ctx")
    e = lax.axis_index("exp")
    return lax.div(c, 2), lax.rem(c, 2), lax.div(e, 4), lax.rem(e, 4)


def up_down(z, core):
    up = lax.rem(z + 1, RING) * 2 + core
    down = lax.rem(z + RING - 1, RING) * 2 + core
    return up, down


def remote(src, dst, send, recv, device):
    return pltpu.make_async_remote_copy(
        src_ref=src,
        dst_ref=dst,
        send_sem=send,
        recv_sem=recv,
        device_id=device,
        device_id_type=MESH,
    )


def conv_part(src_ref, halo, weight_ref, pad_ref):
    count = src_ref.shape[0]
    pad_ref[0:8, :] = halo.astype(F32)
    pad_ref[8 : 8 + count, :] = src_ref[...].astype(F32)
    total = weight_ref[0:1, :] * pad_ref[5 : 5 + count, :]
    for k in range(1, KCONV):
        total = total + weight_ref[k : k + 1, :] * pad_ref[5 + k : 5 + k + count, :]
    return silu(total).astype(BF16)


def expander():
    row = lax.broadcasted_iota(jnp.int32, (HEADS, WIDTH), 0)
    lane = lax.broadcasted_iota(jnp.int32, (HEADS, WIDTH), 1)
    return (lax.div(lane, HDIM) == row).astype(F32)


def spread_cols(values, expand):
    return lax.dot_general(
        values, expand, (((0,), (0,)), ((), ())), precision=HIGH, preferred_element_type=F32
    )


def spread_row(column, expand):
    return jnp.sum(column * expand, axis=0, keepdims=True)


def prepare_kernel(
    x_ref,
    cpl_ref,
    halo_ref,
    step_ref,
    cw_ref,
    cc_ref,
    decay_ref,
    inner_ref,
    coup_ref,
    steps_ref,
    cums_ref,
    first_ref,
    run_ref,
    reach_ref,
    drop_ref,
    pad_ref,
    padc_ref,
):
    inner_ref[...] = conv_part(x_ref, halo_ref[:, :WIDTH], cw_ref, pad_ref)
    coup_ref[...] = conv_part(cpl_ref, halo_ref[:, WIDTH:], cc_ref, padc_ref)
    raw = step_ref[...]
    steps = jnp.maximum(raw, 0.0) + jnp.log1p(jnp.exp(-jnp.abs(raw)))
    steps_ref[...] = steps
    rate = steps * (-jnp.exp(decay_ref[...]))
    row = lax.broadcasted_iota(jnp.int32, (SPAN, SPAN), 0)
    col = lax.broadcasted_iota(jnp.int32, (SPAN, SPAN), 1)
    upper = (row <= col).astype(F32)
    expand = expander()
    states = []
    drops = []
    for b in range(COUNT // SPAN):
        part = slice(b * SPAN, (b + 1) * SPAN)
        cums = jnp.dot(rate[:, part], upper, precision=HIGH, preferred_element_type=F32)
        cums_ref[:, part] = cums
        last = cums[:, SPAN - 1 : SPAN]
        tail = jnp.exp(last - cums) * steps[:, part]
        weighted = (inner_ref[part, :].astype(F32) * spread_cols(tail, expand)).astype(BF16)
        states.append(
            lax.dot_general(
                coup_ref[part, :STATE],
                weighted,
                (((0,), (0,)), ((), ())),
                preferred_element_type=F32,
            )
        )
        drops.append(spread_row(jnp.exp(last), expand))
    first_ref[...] = states[0]
    run_ref[...] = drops[1] * states[0] + states[1]
    reach_ref[...] = drops[0] * drops[1]
    drop_ref[...] = drops[0]


def mixer_kernel(
    inner_ref,
    coup_ref,
    steps_ref,
    cums_ref,
    first_ref,
    drop_ref,
    entry_ref,
    gate_ref,
    skip_ref,
    gain_ref,
    byx_ref,
    byy_ref,
    squares_ref,
    mixed_ref,
):
    expand = expander()
    row = lax.broadcasted_iota(jnp.int32, (SPAN, SPAN), 0)
    col = lax.broadcasted_iota(jnp.int32, (SPAN, SPAN), 1)
    above = row >= col
    lane = lax.broadcasted_iota(jnp.int32, (SPAN, 2 * HDIM), 1)
    for b in range(COUNT // SPAN):
        part = slice(b * SPAN, (b + 1) * SPAN)
        inputs = coup_ref[part, :STATE]
        outputs = coup_ref[part, STATE:]
        scores = lax.dot_general(
            outputs, inputs, (((1,), (1,)), ((), ())), preferred_element_type=F32
        )
        scores = jnp.where(above, scores, 0.0)
        cums = cums_ref[:, part]
        turned = cums.T
        entry = entry_ref[...]
        if b == 1:
            entry = drop_ref[...] * entry + first_ref[...]
        carried = jnp.dot(outputs, entry.astype(BF16), preferred_element_type=F32)
        carried = carried * spread_cols(jnp.exp(cums), expand)
        for pair in range(HEADS // 2):
            cols = slice(pair * 2 * HDIM, (pair + 1) * 2 * HDIM)
            values = inner_ref[part, cols]
            halves = []
            for h in (2 * pair, 2 * pair + 1):
                spread = turned[:, h : h + 1] - cums[h : h + 1, :]
                decay = jnp.exp(jnp.where(above, spread, 0.0))
                mixing = (scores * decay * steps_ref[h : h + 1, part]).astype(BF16)
                halves.append(jnp.dot(mixing, values, preferred_element_type=F32))
            local = jnp.where(lane < HDIM, halves[0], halves[1])
            mixed = local + carried[:, cols] + skip_ref[:, cols] * values.astype(F32)
            mixed_ref[part, cols] = mixed * silu(gate_ref[part, cols].astype(F32))
    gated = mixed_ref[...]
    squares_ref[...] = lax.dot_general(
        jnp.ones((8, WIDTH), F32),
        gated * gated,
        (((1,), (1,)), ((), ())),
        precision=HIGH,
        preferred_element_type=F32,
    )[0:1, :]
    scaled = (gated * gain_ref[...]).astype(BF16)
    byx_ref[...] = scaled
    for x in range(4):
        for y in range(4):
            byy_ref[(y * 4 + x) * TOK : (y * 4 + x + 1) * TOK, :] = scaled[
                (x * 4 + y) * TOK : (x * 4 + y + 1) * TOK, :
            ]


def chain_kernel(
    run_ref,
    reach_ref,
    wi_ref,
    entry_ref,
    iu1_ref,
    id1_ref,
    mine,
    theirs,
    their_reach,
    arriving,
    onward,
    hop_send,
    hop_recv,
    pair_send,
    pair_recv,
    chain_send,
    chain_recv,
    relay_send,
):
    z, core, _, _ = where_am_i()
    up, down = up_down(z, core)
    partner = z * 2 + 1 - core
    barrier = pltpu.get_barrier_semaphore()
    for other in (partner, up, down):
        pl.semaphore_signal(barrier, inc=1, device_id={"ctx": other}, device_id_type=MESH)
    pl.semaphore_wait(barrier, 3)

    hops = [
        remote(wi_ref, iu1_ref, hop_send.at[0], hop_recv.at[0], {"ctx": up}),
        remote(wi_ref, id1_ref, hop_send.at[1], hop_recv.at[1], {"ctx": down}),
    ]
    pairs = [
        remote(mine, theirs, pair_send.at[0], pair_recv.at[0], {"ctx": partner}),
        remote(reach_ref, their_reach, pair_send.at[1], pair_recv.at[1], {"ctx": partner}),
    ]
    rows = STATE // CHUNKS
    spans = [pl.ds(i * rows, rows) for i in range(CHUNKS)]
    ahead = [
        remote(onward.at[s], arriving.at[s], chain_send.at[i], chain_recv.at[i], {"ctx": up})
        for i, s in enumerate(spans)
    ]
    relays = [
        remote(arriving.at[s], arriving.at[s], relay_send.at[i], chain_recv.at[i], {"ctx": partner})
        for i, s in enumerate(spans)
    ]

    @pl.when(core == 0)
    def _():
        mine[...] = run_ref[...].astype(BF16)
        for copy in pairs:
            copy.start()
        for copy in hops:
            copy.start()

        @pl.when(z == 0)
        def _():
            entry_ref[...] = jnp.zeros_like(entry_ref)

        @pl.when(z > 0)
        def _():
            for i, s in enumerate(spans):
                relays[i].wait_recv()
                entry_ref[s, :] = arriving[s, :].astype(F32)

        for copy in pairs:
            copy.wait_send()

    @pl.when(core == 1)
    def _():
        for copy in hops:
            copy.start()
        for copy in pairs:
            copy.wait_recv()

        @pl.when(z == 0)
        def _():
            for i, s in enumerate(spans):
                before = theirs[s, :].astype(F32)
                onward[s, :] = (reach_ref[...] * before + run_ref[s, :]).astype(BF16)
                ahead[i].start()
                entry_ref[s, :] = before

        @pl.when(z > 0)
        def _():
            for i, s in enumerate(spans):
                before = theirs[s, :].astype(F32)
                ahead[i].wait_recv()
                inside = their_reach[...] * arriving[s, :].astype(F32) + before
                onward[s, :] = (reach_ref[...] * inside + run_ref[s, :]).astype(BF16)

                @pl.when(z < RING - 1)
                def _():
                    ahead[i].start()

                relays[i].start()
                entry_ref[s, :] = inside

            for copy in relays:
                copy.wait_send()

        @pl.when(z < RING - 1)
        def _():
            for copy in ahead:
                copy.wait_send()

    for copy in hops:
        copy.wait()


def project_kernel(
    byx_ref,
    byy_ref,
    w_ref,
    squares_ref,
    iu1_ref,
    id1_ref,
    owned_ref,
    sums_ref,
    iu2_ref,
    id2_ref,
    iu3_ref,
    id3_ref,
    parts,
    near,
    far,
    joined,
    near_sum,
    far_sum,
    all_squares,
    ring_send,
    ring_recv,
    sq_send,
    sq_recv,
    hop_send,
    hop_recv,
):
    z, core, x, y = where_am_i()
    up, down = up_down(z, core)
    me = x * 4 + y
    half = D // 2
    quarter = half // 2

    def peer(i):
        return lax.rem(me + i, FLIGHT)

    barrier = pltpu.get_barrier_semaphore()
    for other in (up, down):
        pl.semaphore_signal(barrier, inc=1, device_id={"ctx": other}, device_id_type=MESH)

    def greet(i, carry):
        pl.semaphore_signal(barrier, inc=1, device_id={"exp": peer(i)}, device_id_type=MESH)
        return carry

    lax.fori_loop(1, FLIGHT, greet, 0)
    pl.semaphore_wait(barrier, FLIGHT + 1)

    hops = [
        remote(iu1_ref, iu2_ref, hop_send.at[0], hop_recv.at[0], {"ctx": up}),
        remote(id1_ref, id2_ref, hop_send.at[1], hop_recv.at[1], {"ctx": down}),
        remote(iu2_ref, iu3_ref, hop_send.at[2], hop_recv.at[2], {"ctx": up}),
        remote(id2_ref, id3_ref, hop_send.at[3], hop_recv.at[3], {"ctx": down}),
    ]
    hops[0].start()
    hops[1].start()

    def squares_copy(i):
        return remote(
            squares_ref, all_squares.at[i], sq_send.at[i], sq_recv.at[i], {"exp": peer(i)}
        )

    def send_squares(i, carry):
        squares_copy(i).start()
        return carry

    lax.fori_loop(1, FLIGHT, send_squares, 0)

    def along_x(by):
        return {"exp": lax.rem(x + by, 4) * 4 + y}

    def along_y(by):
        return {"exp": x * 4 + lax.rem(y + by, 4)}

    low = pl.ds(0, quarter)
    high = pl.ds(quarter, quarter)

    def message(stage, side, number, src):
        slot = stage * 12 + side * 6 + number
        toward = along_x if side == stage else along_y
        landing = (near if stage == 0 else far).at[side, number]
        return remote(
            src,
            landing,
            ring_send.at[slot],
            ring_recv.at[slot],
            toward(1 if number % 2 == 0 else 3),
        )

    def block(stage, side, offset):
        if stage == 0:
            return parts.at[side, offset]
        place = y if side == 0 else x
        start = pl.multiple_of(lax.rem(place + offset, 4) * TOK, TOK)
        return joined.at[side, pl.ds(start, TOK)]

    def sources(stage, side):
        across = block(stage, side, 2)
        right = block(stage, side, 1)
        left = block(stage, side, 3)
        sums = near_sum if stage == 0 else far_sum
        return [
            across.at[:, low],
            across.at[:, high],
            right.at[:, high],
            left.at[:, low],
            sums.at[side, 0],
            sums.at[side, 1],
        ]

    copies = [
        [
            [message(stage, side, n, src) for n, src in enumerate(sources(stage, side))]
            for side in range(2)
        ]
        for stage in range(2)
    ]

    def multiply(side, offset):
        rows_ref = byx_ref if side == 0 else byy_ref
        place = x if side == 0 else y
        start = pl.multiple_of(lax.rem(place + offset, 4) * 128, 128)
        rows = rows_ref[pl.ds(start, 128), :]

        def one(i, carry):
            source = pl.ds(pl.multiple_of(side * half + i * 512, 512), 512)
            target = pl.ds(pl.multiple_of(i * 512, 512), 512)
            parts[side, offset, :, target] = jnp.dot(
                rows, w_ref[:, source], preferred_element_type=F32
            ).astype(BF16)
            return carry

        lax.fori_loop(0, half // 512, one, 0)

    def pass_on(stage, side):
        landing = near if stage == 0 else far
        sums = near_sum if stage == 0 else far_sum
        copies[stage][side][0].wait_recv()
        sums[side, 0] = (
            block(stage, side, 1)[:, low].astype(F32) + landing[side, 0].astype(F32)
        ).astype(BF16)
        copies[stage][side][4].start()
        copies[stage][side][1].wait_recv()
        sums[side, 1] = (
            block(stage, side, 3)[:, high].astype(F32) + landing[side, 1].astype(F32)
        ).astype(BF16)
        copies[stage][side][5].start()

    def collect(stage, side):
        landing = near if stage == 0 else far
        for n in (2, 3, 4, 5):
            copies[stage][side][n].wait_recv()
        own = block(stage, side, 0)
        first = own[:, low].astype(F32) + landing[side, 4].astype(F32)
        first = first + landing[side, 3].astype(F32)
        second = own[:, high].astype(F32) + landing[side, 2].astype(F32)
        second = second + landing[side, 5].astype(F32)
        return first, second

    for side in range(2):
        multiply(side, 2)
        copies[0][side][0].start()
        copies[0][side][1].start()
    for side in range(2):
        multiply(side, 1)
        copies[0][side][2].start()
        multiply(side, 3)
        copies[0][side][3].start()
    for side in range(2):
        pass_on(0, side)
    for side in range(2):
        multiply(side, 0)
    for side in range(2):
        first, second = collect(0, side)
        joined[side, :, low] = first.astype(BF16)
        joined[side, :, high] = second.astype(BF16)
        for n in range(4):
            copies[1][side][n].start()
    hops[0].wait_recv()
    hops[2].start()
    hops[1].wait_recv()
    hops[3].start()
    for side in range(2):
        pass_on(1, side)
    for side in range(2):
        first, second = collect(1, side)
        owned_ref[:, pl.ds(side * half, quarter)] = first
        owned_ref[:, pl.ds(side * half + quarter, quarter)] = second

    all_squares[0] = squares_ref[...]

    def take_squares(i, carry):
        squares_copy(i).wait()
        return carry

    lax.fori_loop(1, FLIGHT, take_squares, 0)
    total = all_squares[0]
    for i in range(1, FLIGHT):
        total = total + all_squares[i]
    sums_ref[...] = total

    for stage in range(2):
        for side in range(2):
            for copy in copies[stage][side]:
                copy.wait_send()
    hops[0].wait_send()
    hops[1].wait_send()
    hops[2].wait()
    hops[3].wait()


def route_kernel(
    owned_ref,
    sums_ref,
    residual_ref,
    gain_ref,
    router_ref,
    routes_ref,
    priority_ref,
    hidden_ref,
    rows_ref,
    weights_ref,
):
    me = lax.axis_index("exp")
    row = lax.broadcasted_iota(jnp.int32, (TOK, COUNT), 0)
    col = lax.broadcasted_iota(jnp.int32, (TOK, COUNT), 1)
    squares = jnp.sum(
        jnp.where(col == me * TOK + row, sums_ref[...], 0.0), axis=1, keepdims=True
    )
    hidden = residual_ref[...].astype(F32) + owned_ref[...] * lax.rsqrt(squares / INNER + EPS)
    hidden_ref[...] = hidden
    mean = jnp.sum(hidden * hidden, axis=1, keepdims=True) / D
    normed = (hidden * lax.rsqrt(mean + EPS) * gain_ref[...]).astype(BF16)
    logits = jnp.dot(normed, router_ref[...], preferred_element_type=F32)
    expert = lax.broadcasted_iota(jnp.int32, (TOK, NEXP), 1)
    named = expert < 0
    for k in range(TOPK):
        named = named | (routes_ref[:, k : k + 1] == expert)
    raised = jnp.where(named, jnp.exp(logits), 0.0)
    share = (raised / jnp.sum(raised, axis=1, keepdims=True)).astype(BF16)
    member = named.astype(F32).astype(BF16)
    square_row = lax.broadcasted_iota(jnp.int32, (TOK, TOK), 0)
    square_col = lax.broadcasted_iota(jnp.int32, (TOK, TOK), 1)
    order = priority_ref[...].astype(F32)
    own_order = jnp.sum(jnp.where(square_row == square_col, order, 0.0), axis=1, keepdims=True)
    earlier = (order < own_order).astype(F32).astype(BF16)
    rank = jnp.dot(earlier, member, preferred_element_type=F32)
    key = jnp.where(named, rank, 99.0).astype(BF16)
    lanes = FLIGHT * CAP
    wide_row = lax.broadcasted_iota(jnp.int32, (NEXP, lanes), 0)
    wide_col = lax.broadcasted_iota(jnp.int32, (NEXP, lanes), 1)
    widen = (lax.div(wide_col, CAP) == wide_row).astype(F32).astype(BF16)
    key_wide = jnp.dot(key, widen, preferred_element_type=F32)
    share_wide = jnp.dot(share, widen, preferred_element_type=F32)
    slot = lax.rem(lax.broadcasted_iota(jnp.int32, (TOK, lanes), 1), CAP).astype(F32)
    chosen = (key_wide == slot).astype(F32)
    weights_ref[...] = (chosen * share_wide).astype(BF16)
    pick = chosen.astype(BF16)
    for s in range(2 * RING):
        taken = lax.dot_general(
            pick,
            normed[:, s * SLICE : (s + 1) * SLICE],
            (((0,), (0,)), ((), ())),
            preferred_element_type=F32,
        )
        rows_ref[s % 2, :, :, (s // 2) * SLICE : (s // 2 + 1) * SLICE] = taken.reshape(
            FLIGHT, CAP, SLICE
        ).astype(BF16)


def expert_kernel(
    rows_ref,
    wi_ref,
    iu1_ref,
    id1_ref,
    iu2_ref,
    id2_ref,
    iu3_ref,
    id3_ref,
    wo_ref,
    back_ref,
    landed,
    tokens,
    weights,
    downs,
    units,
    units_out,
    units_in,
    answers,
    row_send,
    row_recv,
    back_send,
    back_recv,
    hop_send,
    hop_recv,
    load_sem,
    own_sem,
    pair_send,
    pair_recv,
):
    z, core, x, y = where_am_i()
    up, down = up_down(z, core)
    me = x * 4 + y
    partner = z * 2 + 1 - core
    plane = 2 * FLIGHT

    def peer(i):
        other = lax.rem(me + lax.div(i, 2), FLIGHT)
        other_core = lax.rem(core + i, 2)
        return other, other_core, {"ctx": z * 2 + other_core, "exp": other}

    barrier = pltpu.get_barrier_semaphore()
    for other in (up, down):
        pl.semaphore_signal(barrier, inc=1, device_id={"ctx": other}, device_id_type=MESH)

    def greet(i, carry):
        pl.semaphore_signal(barrier, inc=1, device_id=peer(i)[2], device_id_type=MESH)
        return carry

    lax.fori_loop(1, plane, greet, 0)
    pl.semaphore_wait(barrier, plane + 1)

    pieces = [wi_ref, iu1_ref, iu2_ref, iu3_ref, id1_ref, id2_ref, id3_ref]
    half = SLICE // 2
    hops = [
        remote(
            iu3_ref.at[pl.ds(0, half)],
            weights.at[7, pl.ds(0, half)],
            hop_send.at[0],
            hop_recv.at[0],
            {"ctx": up},
        ),
        remote(
            id3_ref.at[pl.ds(half, half)],
            weights.at[7, pl.ds(half, half)],
            hop_send.at[1],
            hop_recv.at[1],
            {"ctx": down},
        ),
    ]
    for n in range(3):
        src_up = wo_ref if n == 0 else downs.at[n]
        src_down = wo_ref if n == 0 else downs.at[3 + n]
        hops.append(
            remote(
                src_up, downs.at[n + 1], hop_send.at[2 * n + 2], hop_recv.at[2 * n + 2], {"ctx": up}
            )
        )
        hops.append(
            remote(
                src_down,
                downs.at[n + 4],
                hop_send.at[2 * n + 3],
                hop_recv.at[2 * n + 3],
                {"ctx": down},
            )
        )
    hops.append(
        remote(
            downs.at[3, pl.ds(0, half)],
            downs.at[7, pl.ds(0, half)],
            hop_send.at[8],
            hop_recv.at[8],
            {"ctx": up},
        )
    )
    hops.append(
        remote(
            downs.at[6, pl.ds(half, half)],
            downs.at[7, pl.ds(half, half)],
            hop_send.at[9],
            hop_recv.at[9],
            {"ctx": down},
        )
    )

    def row_copy(i):
        other, other_core, device = peer(i)
        return remote(
            rows_ref.at[other_core, other],
            landed.at[me, core],
            row_send.at[i],
            row_recv.at[i],
            device,
        )

    def start_rows(i, carry):
        row_copy(i).start()
        return carry

    lax.fori_loop(1, plane, start_rows, 0)
    for n in range(4):
        hops[n].start()
    own_rows = pltpu.make_async_copy(rows_ref.at[core, me], landed.at[me, core], own_sem.at[0])
    own_rows.start()
    loads = [
        pltpu.make_async_copy(piece, weights.at[n], load_sem.at[n]) for n, piece in enumerate(pieces)
    ]
    own_down = pltpu.make_async_copy(wo_ref, downs.at[0], own_sem.at[1])
    for copy in loads:
        copy.start()
    own_down.start()

    own_rows.wait()

    def take_rows(i, carry):
        row_copy(i).wait()
        return carry

    lax.fori_loop(1, plane, take_rows, 0)

    for s in range(RING):
        block = landed[:, :, :, s * SLICE : (s + 1) * SLICE].astype(F32)
        tokens[s] = block.reshape(plane * CAP, SLICE).astype(BF16)

    def source(n):
        if n <= 3:
            return lax.rem(z + RING - n, RING)
        if n <= 6:
            return lax.rem(z + n - 3, RING)
        return lax.rem(z + 4, RING)

    def forward(n):
        hops[n].wait_recv()
        hops[n + 2].start()

    for copy in loads:
        copy.wait()
    forward(2)
    forward(3)

    def gate_up(i, carry):
        cols = pl.ds(pl.multiple_of(i * 256, 256), 256)
        total = jnp.dot(tokens[source(0)], weights[0, :, cols], preferred_element_type=F32)
        for n in range(1, 7):
            total = total + jnp.dot(
                tokens[source(n)], weights[n, :, cols], preferred_element_type=F32
            )
        units[:, cols] = total
        return carry

    lax.fori_loop(0, 2 * FFE // 256, gate_up, 0)
    hops[0].wait_recv()
    hops[1].wait_recv()

    def last_slice(i, carry):
        cols = pl.ds(pl.multiple_of(i * 256, 256), 256)
        total = units[:, cols] + jnp.dot(
            tokens[source(7)], weights[7, :, cols], preferred_element_type=F32
        )
        units[:, cols] = total
        units_out[:, cols] = total.astype(BF16)
        return carry

    lax.fori_loop(0, 2 * FFE // 256, last_slice, 0)
    swap = remote(units_out, units_in, pair_send.at[0], pair_recv.at[0], {"ctx": partner})
    swap.start()
    swap.wait()
    gate = units[:, :FFE] + units_in[:, :FFE].astype(F32)
    lift = units[:, FFE:] + units_in[:, FFE:].astype(F32)
    activated = (silu(gate) * lift).astype(BF16)
    own_down.wait()

    def answer(n):
        values = lax.dot_general(
            activated, downs[n], (((1,), (1,)), ((), ())), preferred_element_type=F32
        )
        cols = pl.ds(pl.multiple_of(source(n) * SLICE, SLICE), SLICE)
        answers[:, :, :, cols] = values.reshape(FLIGHT, 2, CAP, SLICE).astype(BF16)

    answer(0)
    answer(1)
    answer(4)
    forward(4)
    forward(5)
    answer(2)
    answer(5)
    hops[6].wait_recv()
    hops[8].start()
    hops[7].wait_recv()
    hops[9].start()
    answer(3)
    answer(6)
    hops[8].wait_recv()
    hops[9].wait_recv()
    answer(7)

    def back_copy(i):
        other, other_core, device = peer(i)
        return remote(
            answers.at[other, other_core],
            back_ref.at[me, core],
            back_send.at[i],
            back_recv.at[i],
            device,
        )

    def start_back(i, carry):
        back_copy(i).start()
        return carry

    lax.fori_loop(1, plane, start_back, 0)
    own_back = pltpu.make_async_copy(answers.at[me, core], back_ref.at[me, core], own_sem.at[2])
    own_back.start()
    own_back.wait()

    def take_back(i, carry):
        back_copy(i).wait()
        return carry

    lax.fori_loop(1, plane, take_back, 0)
    for copy in hops:
        copy.wait_send()


def combine_kernel(weights_ref, back_ref, out_ref):
    weights = weights_ref[...]
    for j in range(2):
        rows = back_ref[:, j].astype(F32).reshape(FLIGHT * CAP, D // 2).astype(BF16)
        total = jnp.dot(weights, rows, preferred_element_type=F32)
        for s in range(RING):
            place = (2 * s + j) * SLICE
            out_ref[:, place : place + SLICE] = total[:, s * SLICE : (s + 1) * SLICE]


def call(kernel, outs, in_specs, out_specs, scratch=(), collective_id=None):
    if collective_id is None:
        params = pltpu.CompilerParams(vmem_limit_bytes=VMEM_LIMIT)
    else:
        params = pltpu.CompilerParams(
            vmem_limit_bytes=VMEM_LIMIT, collective_id=collective_id, has_side_effects=True
        )
    return pl.pallas_call(
        kernel,
        out_shape=outs,
        in_specs=in_specs,
        out_specs=out_specs,
        scratch_shapes=list(scratch),
        compiler_params=params,
    )


def body(
    inner_input,
    gate_input,
    coupling_input,
    step_input,
    conv_inner,
    conv_coupling,
    decay_log,
    skip_gain,
    norm_gain,
    out_weight,
    residual,
    moe_gain,
    router_weight,
    routes,
    priority,
    expert_in,
    expert_out,
):
    devices = lax.axis_size("ctx")
    edges = jnp.concatenate([inner_input[COUNT - 8 :], coupling_input[COUNT - 8 :]], axis=1)
    halo = lax.ppermute(edges, "ctx", [(i, i + 1) for i in range(devices - 1)])
    wi = expert_in[0]
    wo = expert_out[0]
    dma = pltpu.SemaphoreType.DMA

    inner, coup, steps, cums, first, run, reach, drop = call(
        prepare_kernel,
        (
            shaped((COUNT, WIDTH), BF16),
            shaped((COUNT, 2 * STATE), BF16),
            shaped((HEADS, COUNT), F32),
            shaped((HEADS, COUNT), F32),
            shaped((STATE, WIDTH), F32),
            shaped((STATE, WIDTH), F32),
            shaped((1, WIDTH), F32),
            shaped((1, WIDTH), F32),
        ),
        [vmem()] * 7,
        [vmem()] * 8,
        [pltpu.VMEM((COUNT + 8, WIDTH), F32), pltpu.VMEM((COUNT + 8, 2 * STATE), F32)],
    )(
        inner_input,
        coupling_input,
        halo,
        step_input.T,
        conv_inner,
        conv_coupling,
        decay_log[:, None],
    )

    piece = shaped((SLICE, 2 * FFE), BF16)
    entry, iu1, id1 = call(
        chain_kernel,
        (shaped((STATE, WIDTH), F32), piece, piece),
        [vmem(), vmem(), anyspace()],
        [vmem(), anyspace(), anyspace()],
        [
            pltpu.VMEM((STATE, WIDTH), BF16),
            pltpu.VMEM((STATE, WIDTH), BF16),
            pltpu.VMEM((1, WIDTH), F32),
            pltpu.VMEM((STATE, WIDTH), BF16),
            pltpu.VMEM((STATE, WIDTH), BF16),
            dma((2,)),
            dma((2,)),
            dma((2,)),
            dma((2,)),
            dma((CHUNKS,)),
            dma((CHUNKS,)),
            dma((CHUNKS,)),
        ],
        collective_id=0,
    )(run, reach, wi)

    byx, byy, squares = call(
        mixer_kernel,
        (
            shaped((COUNT, WIDTH), BF16),
            shaped((COUNT, WIDTH), BF16),
            shaped((1, COUNT), F32),
        ),
        [vmem()] * 10,
        [vmem()] * 3,
        [pltpu.VMEM((COUNT, WIDTH), F32)],
    )(
        inner,
        coup,
        steps,
        cums,
        first,
        drop,
        entry,
        gate_input,
        jnp.repeat(skip_gain, HDIM)[None, :],
        norm_gain[None, :],
    )

    owned, sums, iu2, id2, iu3, id3 = call(
        project_kernel,
        (shaped((TOK, D), F32), shaped((1, COUNT), F32), piece, piece, piece, piece),
        [vmem()] * 4 + [anyspace()] * 2,
        [vmem()] * 2 + [anyspace()] * 4,
        [
            pltpu.VMEM((2, 4, 128, D // 2), BF16),
            pltpu.VMEM((2, 6, 128, D // 4), BF16),
            pltpu.VMEM((2, 6, TOK, D // 4), BF16),
            pltpu.VMEM((2, 128, D // 2), BF16),
            pltpu.VMEM((2, 2, 128, D // 4), BF16),
            pltpu.VMEM((2, 2, TOK, D // 4), BF16),
            pltpu.VMEM((FLIGHT, 1, COUNT), F32),
            dma((24,)),
            dma((24,)),
            dma((FLIGHT,)),
            dma((FLIGHT,)),
            dma((4,)),
            dma((4,)),
        ],
        collective_id=1,
    )(byx, byy, out_weight, squares, iu1, id1)

    hidden, rows, weights = call(
        route_kernel,
        (
            shaped((TOK, D), F32),
            shaped((2, FLIGHT, CAP, D // 2), BF16),
            shaped((TOK, FLIGHT * CAP), BF16),
        ),
        [vmem()] * 7,
        [vmem()] * 3,
    )(owned, sums, residual, moe_gain[None, :], router_weight, routes, priority)

    back = call(
        expert_kernel,
        shaped((FLIGHT, 2, CAP, D // 2), BF16),
        [vmem()] + [anyspace()] * 8,
        anyspace(),
        [
            pltpu.VMEM((FLIGHT, 2, CAP, D // 2), BF16),
            pltpu.VMEM((RING, 2 * FLIGHT * CAP, SLICE), BF16),
            pltpu.VMEM((RING, SLICE, 2 * FFE), BF16),
            pltpu.VMEM((RING, SLICE, FFE), BF16),
            pltpu.VMEM((2 * FLIGHT * CAP, 2 * FFE), F32),
            pltpu.VMEM((2 * FLIGHT * CAP, 2 * FFE), BF16),
            pltpu.VMEM((2 * FLIGHT * CAP, 2 * FFE), BF16),
            pltpu.VMEM((FLIGHT, 2, CAP, D // 2), BF16),
            dma((2 * FLIGHT,)),
            dma((2 * FLIGHT,)),
            dma((2 * FLIGHT,)),
            dma((2 * FLIGHT,)),
            dma((10,)),
            dma((10,)),
            dma((7,)),
            dma((3,)),
            dma((1,)),
            dma((1,)),
        ],
        collective_id=2,
    )(rows, wi, iu1, id1, iu2, id2, iu3, id3, wo)

    moe_out = call(
        combine_kernel, shaped((TOK, D), F32), [vmem()] * 2, vmem()
    )(weights, back)
    return (hidden, moe_out)


def solution(mesh):
    placed = (
        P("ctx", "exp"),
        P("ctx", "exp"),
        P("ctx", None),
        P("ctx", "exp"),
        P(None, "exp"),
        P(),
        P("exp"),
        P("exp"),
        P("exp"),
        P("exp", None),
        P(("ctx", "exp"), None),
        P(),
        P(),
        P(("ctx", "exp"), None),
        P(("ctx", "exp"), None),
        P("exp", "ctx", None),
        P("exp", "ctx", None),
    )
    return jax.shard_map(
        body,
        mesh=mesh,
        in_specs=placed,
        out_specs=(P(("ctx", "exp"), None), P(("ctx", "exp"), None)),
        check_vma=False,
    )
```

time: 356 us -> 182 us (0.51)
  waiting for transfers between devices: 209 us -> 0.01 us
  Pallas kernels: 0 us -> 168 us
  blocking collectives: 69.2 us -> 0 us
  matrix products: 25 us -> 0 us
  between operations: 14.8 us -> 0.67 us
  other arithmetic: 13 us -> 0.01 us
  starting transfers between devices: 11.6 us -> 4.91 us
    pallas_call x0 -> x7, Pallas kernels: none -> 168 us  [the longest x1 65.1 us: body(): call(expert_kernel, shaped((FLIGHT, 2, CAP, D // 2), BF16), [vmem()] + [a...]
    all_gather x3 -> x0, waiting for transfers between devices: 121 us -> none  [the longest x1 59.4 us: body(): whole_in = lax.all_gather(expert_in[0], 'ctx', axis=0, tiled=True)]
    reduce_scatter x1 -> x0, waiting for transfers between devices: 70.9 us -> none  [body(): lax.psum_scatter(projected.astype(jnp.bfloat16), 'exp', scatter_dimension...]
    unnamed x1 -> x0, blocking collectives: 32.9 us -> none
    dot_general x9 -> x0, matrix products: 23.5 us -> none  [the longest x1 6.61 us: body(): jnp.einsum('rkw,kwf->krf', rows.reshape(rows.shape[0], slices, slice_widt...]
    all_gather x1 -> x0, blocking collectives: 18.8 us -> none  [carried_in(): gathered = jax.tree.map(lambda a: lax.all_gather(a, axis), part)]
    all_to_all x1 -> x0, blocking collectives: 17.5 us -> none  [body(): lax.all_to_all(outbound, 'exp', split_axis=0, concat_axis=0, tiled=True)]
    all_to_all x1 -> x0, waiting for transfers between devices: 15.2 us -> none  [body(): lax.all_to_all(answer.reshape(flight, capacity, answer.shape[1]), 'exp',...]
  transfers between devices with their start and end apart: 6 -> 1, of which waited for: 5 -> 0; matrix products, arithmetic and copies ran while one was open for 6% -> 3% of each run, Pallas kernels for 0% -> 0%
where the time goes in v1:
time: 182 us
  Pallas kernels  168 us (92%)
  local copies, waits for them, and re-layouts  8.25 us (5%)
  starting transfers between devices  4.91 us (3%)
    pallas_call x1, Pallas kernels, body(): call(expert_kernel, shaped((FLIGHT, 2, CAP, D // 2), BF16), [vmem()] + [a...  65.1 us
    pallas_call x1, Pallas kernels, body(): call(project_kernel, (shaped((TOK, D), F32), shaped((1, COUNT), F32), pie...  61.2 us
    pallas_call x1, Pallas kernels, body(): call(chain_kernel, (shaped((STATE, WIDTH), F32), piece, piece), [vmem(),...  25.4 us
    pallas_call x1, Pallas kernels, body(): call(prepare_kernel, (shaped((COUNT, WIDTH), BF16), shaped((COUNT, 2 * ST...  5.25 us
    pallas_call x1, Pallas kernels, body(): call(mixer_kernel, (shaped((COUNT, WIDTH), BF16), shaped((COUNT, WIDTH),...  4.92 us
    ppermute x1, starting transfers between devices, body(): halo = lax.ppermute(edges, 'ctx', [(i, i + 1) for i in range(devices - 1)])  4.91 us
    unnamed x4, local copies, waits for them, and re-layouts  4.16 us
    pallas_call x1, Pallas kernels, body(): call(route_kernel, (shaped((TOK, D), F32), shaped((2, FLIGHT, CAP, D // 2...  3.72 us
  transfers between devices with their start and end apart: 1, of which 0 were waited for; matrix products, arithmetic and copies ran while one was open for 3% of the time, Pallas kernels for 0%

profile of v1, /device:TPU:1, one launch (start us, length us, event | category | flops | bytes accessed | tf_op | source)
XLA Modules:
  0.0 181.8 jit_solution(12687205838557440604)
XLA Ops:
  0.6 0.7 slice.7
  1.3 0.7 slice.6
  2.0 4.9 %collective-permute-start = (bf16[8,768]{1,0:T(8,128)(2,1)S(1)}, bf16[8,768]{1,0:T(8,128)(2,1)S(1)}, u32[]{:S(2)}, u32[]{:S(2)}) collective-permute-start(bf16[8,768]{1,0:T(8,128)(2,1)S(1)} %pad_maximum_fusion), channel_id=1, source_target_pairs={{0,16},{16,32},{32,48},{48,64},{64,80},{80,96},{96,112},{112,128},... | collective-permute-start | bytes 36872 | tf_op jit(solution)/shard_map/ppermute | solution.py:890
  6.9 1.3 copy.19.decay_ref
  8.3 0.7 broadcast_in_dim.13
  9.0 0.7 broadcast_in_dim_reshape.3.skip_ref
  9.6 1.4 copy.21.routes_ref
  11.0 2.2 %copy.20.router_ref = bf16[4096,72]{1,0:T(8,128)(2,1)} copy(bf16[4096,72]{0,1:T(8,128)(2,1)} %param.29) | data formatting | bytes 1179648 | tf_op args[12]
  13.2 0.0 collective-permute-done.halo_ref
  13.2 0.0 copy-start
  13.2 0.6 copy-done
  13.8 5.2 %shard_map.176 = (bf16[512,512]{1,0:T(8,128)(2,1)}, bf16[512,256]{1,0:T(8,128)(2,1)}, f32[8,512]{1,0:T(8,128)}, f32[8,512]{1,0:T(8,128)}, f32[128,512]{1,0:T(8,1...) custom-call(bf16[512,512]{1,0:T(8,128)(2,1)} %x_ref.1, bf16[512,256]{1,0:T(8,128)(2,1)} %cpl_ref.1, ...), custom_call_target="tpu_custom_call" | custom-call | tf_op jit(solution)/shard_map/pallas_call | solution.py:895
  19.1 25.4 %shard_map.177 = (f32[128,512]{1,0:T(8,128)}, bf16[256,1536]{1,0:T(8,128)(2,1)}, bf16[256,1536]{1,0:T(8,128)(2,1)}) custom-call(f32[128,512]{1,0:T(8,128)} %get-tuple-element.31.run_ref, f32[1,512]{1,0:T(1,128)} %get-tuple-element.32.reach_ref, bf16[256,1536]{1,0:T(8,128)(2,1)} %bitcast.6), custom_call_target="tpu_custom_call" | custom-call | tf_op jit(solution)/shard_map/pallas_call | solution.py:921
  44.5 4.9 %shard_map.178 = (bf16[512,512]{1,0:T(8,128)(2,1)}, bf16[512,512]{1,0:T(8,128)(2,1)}, f32[1,512]{1,0:T(1,128)}) custom-call(bf16[512,512]{1,0:T(8,128)(2,1)} %get-tuple-element.25.inner_ref, bf16[512,256]{1,0:T(8,128)(2,1)} %get-tuple-element.26.coup_ref, f32[8,512]{1,0:T(8,128)} %get-tuple-element.27.steps_ref, f32[8,512]{1,0:T(8,128)} %get-tuple-element.28.cums_ref, ...), custom_call_target="tpu_custom_call" | custom-call | tf_op jit(solution)/shard_map/pallas_call | solution.py:943
  49.4 61.2 %shard_map.179 = (f32[32,4096]{1,0:T(8,128)}, f32[1,512]{1,0:T(1,128)}, bf16[256,1536]{1,0:T(8,128)(2,1)}, bf16[256,1536]{1,0:T(8,128)(2,1)}, bf16[256,1536]{1,0:T(8,128)(2,1)}, /*index=5*/bf16[256,1536]{1,0:T(8,128)(2,1)}) custom-call(bf16[512,512]{1,0:T(8,128)(2,1)} %get-tuple-element.34.byx_ref, bf16[512,512]{1,0:T(8,128)(2,1)} %get-tuple-element.35.byy_ref, ...), custom_call_target="tpu_custom_call" | custom-call | tf_op jit(solution)/shard_map/pallas_call | solution.py:966
  110.6 3.7 %shard_map.180 = (f32[32,4096]{1,0:T(8,128)}, bf16[2,16,8,2048]{3,2,1,0:T(8,128)(2,1)}, bf16[32,128]{1,0:T(8,128)(2,1)}) custom-call(f32[32,4096]{1,0:T(8,128)} %get-tuple-element.39.owned_ref, f32[1,512]{1,0:T(1,128)} %get-tuple-element.40.sums_ref, bf16[32,4096]{1,0:T(8,128)(2,1)} %residual_ref.1, f32[1,4096]{1,0:T(1,128)} %bitcast.9, ...), custom_call_target="tpu_custom_call" | custom-call | tf_op jit(solution)/shard_map/pallas_call | solution.py:989
  114.3 65.1 %shard_map.181.back_ref = bf16[16,2,8,2048]{3,2,1,0:T(8,128)(2,1)} custom-call(bf16[2,16,8,2048]{3,2,1,0:T(8,128)(2,1)} %get-tuple-element.43.rows_ref, bf16[256,1536]{1,0:T(8,128)(2,1)} %bitcast.7, bf16[256,1536]{1,0:T(8,128)(2,1)} %get-tuple-element.37.iu1_ref, bf16[256,1536]{1,0:T(8,128)(2,1)} %get-tuple-element.38.id1_ref, ...), custom_call_target="tpu_custom_call" | custom-call | tf_op jit(solution)/shard_map/pallas_call | solution.py:1000
  179.5 2.3 %shard_map.182 = f32[32,4096]{1,0:T(8,128)} custom-call(bf16[32,128]{1,0:T(8,128)(2,1)} %get-tuple-element.42.weights_ref, bf16[16,2,8,2048]{3,2,1,0:T(8,128)(2,1)} %shard_map.181.back_ref), custom_call_target="tpu_custom_call" | custom-call | tf_op jit(solution)/shard_map/pallas_call | solution.py:1028
  (1 shorter events, 0.0 us)
Async XLA Ops:
  2.0 11.2 %collective-permute-start = (bf16[8,768]{1,0:T(8,128)(2,1)S(1)}, bf16[8,768]{1,0:T(8,128)(2,1)S(1)}, u32[]{:S(2)}, u32[]{:S(2)}) collective-permute-start(bf16[8,768]{1,0:T(8,128)(2,1)S(1)} %pad_maximum_fusion), channel_id=1, source_target_pairs={{0,16},{16,32},{32,48},{48,64},{64,80},{80,96},{96,112},{112,128},... | collective-permute-start | bytes 36872 | tf_op jit(solution)/shard_map/ppermute | solution.py:890
  13.2 0.6 copy-start

commit v2 on v0

v2 whole, which is shorter than its diff:
```python
from types import SimpleNamespace

import jax
import jax.numpy as jnp
from jax import lax
from jax.experimental import pallas as pl
from jax.experimental.pallas import tpu as pltpu
from jax.sharding import PartitionSpec as P

HDIM = 64
STATE = 128
KCONV = 4
NEXP = 72
TOPK = 10
FFE = 768
SPAN = 256
INNER = 8192
D = 4096
HEADS = 8
WIDTH = 512
COUNT = 512
TOK = 32
CAP = 8
FLIGHT = 16
SLICE = 256
RING = 8
CHUNKS = 8
EDGE = 16
PLANE = 32
GROUPS = ((0, 1, 4, 2), (5, 3, 6, 7))

EPS = 1e-05
HIGH = lax.Precision.HIGHEST
F32 = jnp.float32
BF16 = jnp.bfloat16
MESH = pl.DeviceIdType.MESH
VMEM_LIMIT = 60 * 1024 * 1024


def vmem():
    return pl.BlockSpec(memory_space=pltpu.VMEM)


def anyspace():
    return pl.BlockSpec(memory_space=pl.ANY)


def shaped(shape, dtype):
    return jax.ShapeDtypeStruct(shape, dtype)


def silu(x):
    return x * jax.nn.sigmoid(x)


def where_am_i():
    c = lax.axis_index("ctx")
    e = lax.axis_index("exp")
    return lax.div(c, 2), lax.rem(c, 2), lax.div(e, 4), lax.rem(e, 4)


def up_down(z, core):
    up = lax.rem(z + 1, RING) * 2 + core
    down = lax.rem(z + RING - 1, RING) * 2 + core
    return up, down


def remote(src, dst, send, recv, device):
    return pltpu.make_async_remote_copy(
        src_ref=src,
        dst_ref=dst,
        send_sem=send,
        recv_sem=recv,
        device_id=device,
        device_id_type=MESH,
    )


def conv_part(src_ref, halo, weight_ref, pad_ref):
    count = src_ref.shape[0]
    pad_ref[0:EDGE, :] = halo
    pad_ref[EDGE : EDGE + count, :] = src_ref[...].astype(F32)
    first = EDGE - KCONV + 1
    total = weight_ref[0:1, :] * pad_ref[first : first + count, :]
    for k in range(1, KCONV):
        total = total + weight_ref[k : k + 1, :] * pad_ref[first + k : first + k + count, :]
    return silu(total).astype(BF16)


def expander():
    row = lax.broadcasted_iota(jnp.int32, (HEADS, WIDTH), 0)
    lane = lax.broadcasted_iota(jnp.int32, (HEADS, WIDTH), 1)
    return (lax.div(lane, HDIM) == row).astype(F32)


def spread_cols(values, expand):
    return lax.dot_general(
        values, expand, (((0,), (0,)), ((), ())), precision=HIGH, preferred_element_type=F32
    )


def spread_row(column, expand):
    return jnp.sum(column * expand, axis=0, keepdims=True)


def diagonal(row):
    n = row.shape[1]
    a = lax.broadcasted_iota(jnp.int32, (n, n), 0)
    b = lax.broadcasted_iota(jnp.int32, (n, n), 1)
    return jnp.sum(jnp.where(a == b, row, 0.0), axis=1, keepdims=True)


INPUTS = [
    "x",
    "cpl",
    "step",
    "conv",
    "conv_cpl",
    "decay",
    "skip",
    "norm_gain",
    "moe_gain",
    "routes",
    "priority",
    "gate_in",
    "out_w",
    "residual_in",
    "router_in",
    "wi",
    "wo",
]
OUTPUTS = ["hidden", "moe_out"]


def scratch():
    dma = pltpu.SemaphoreType.DMA
    V = pltpu.VMEM
    half, quarter = D // 2, D // 4
    return {
        "gate": V((COUNT, WIDTH), BF16),
        "w": V((WIDTH, D), BF16),
        "residual": V((TOK, D), BF16),
        "router": V((NEXP, D), BF16),
        "halo_x": V((EDGE, WIDTH), BF16),
        "halo_c": V((EDGE, 2 * STATE), BF16),
        "pad": V((COUNT + EDGE, WIDTH), F32),
        "pad_c": V((COUNT + EDGE, 2 * STATE), F32),
        "inner": V((COUNT, WIDTH), BF16),
        "coup": V((COUNT, 2 * STATE), BF16),
        "steps": V((HEADS, COUNT), F32),
        "cums": V((HEADS, COUNT), F32),
        "first": V((STATE, WIDTH), F32),
        "run": V((STATE, WIDTH), F32),
        "reach": V((1, WIDTH), F32),
        "drop": V((1, WIDTH), F32),
        "entry": V((STATE, WIDTH), F32),
        "gated": V((COUNT, WIDTH), F32),
        "growth": V((COUNT, WIDTH), F32),
        "byx": V((COUNT, WIDTH), BF16),
        "byy": V((COUNT, WIDTH), BF16),
        "squares": V((1, COUNT), F32),
        "sums": V((1, COUNT), F32),
        "mine": V((STATE, WIDTH), BF16),
        "theirs": V((STATE, WIDTH), BF16),
        "their_reach": V((1, WIDTH), F32),
        "arriving": V((STATE, WIDTH), BF16),
        "onward": V((STATE, WIDTH), BF16),
        "parts": V((2, 4, 128, half), BF16),
        "near": V((2, 6, 128, quarter), BF16),
        "far": V((2, 6, TOK, quarter), BF16),
        "joined": V((2, 128, half), BF16),
        "near_sum": V((2, 2, 128, quarter), BF16),
        "far_sum": V((2, 2, TOK, quarter), BF16),
        "all_squares": V((FLIGHT, 1, COUNT), F32),
        "owned": V((TOK, D), F32),
        "normed": V((2 * RING, TOK, SLICE), BF16),
        "share": V((TOK, FLIGHT * CAP), BF16),
        "rows": V((2, 2, FLIGHT, CAP, quarter), BF16),
        "landed": V((2, FLIGHT, 2, CAP, quarter), BF16),
        "tokens": V((RING, PLANE * CAP, SLICE), BF16),
        "ups": V((RING, SLICE, 2 * FFE), BF16),
        "downs": V((RING, SLICE, FFE), BF16),
        "units": V((PLANE * CAP, 2 * FFE), F32),
        "units_out": V((PLANE * CAP, 2 * FFE), BF16),
        "units_in": V((PLANE * CAP, 2 * FFE), BF16),
        "answers": V((2, FLIGHT, 2, CAP, quarter), BF16),
        "back": V((2, FLIGHT, 2, CAP, quarter), BF16),
        "load_sem": dma((6,)),
        "halo_send": dma((2,)),
        "halo_recv": dma((2,)),
        "pair_send": dma((3,)),
        "pair_recv": dma((3,)),
        "chain_send": dma((CHUNKS,)),
        "chain_recv": dma((CHUNKS,)),
        "relay_send": dma((CHUNKS,)),
        "hop_send": dma((17,)),
        "hop_recv": dma((17,)),
        "ring_send": dma((24,)),
        "ring_recv": dma((24,)),
        "sq_send": dma((FLIGHT,)),
        "sq_recv": dma((FLIGHT,)),
        "row_send": dma((2, PLANE)),
        "row_recv": dma((2, PLANE)),
        "back_send": dma((2, PLANE)),
        "back_recv": dma((2, PLANE)),
        "own_sem": dma((4,)),
    }


def layer_kernel(*refs):
    r = SimpleNamespace(**dict(zip(INPUTS + OUTPUTS + list(scratch()), refs, strict=True)))
    z, core, x, y = where_am_i()
    c = z * 2 + core
    me = x * 4 + y
    up, down = up_down(z, core)
    partner = z * 2 + 1 - core
    after = lax.rem(c + 1, 2 * RING)
    before = lax.rem(c + 2 * RING - 1, 2 * RING)
    cross = jnp.where(core == 0, before, after)

    def peer(i):
        return lax.rem(me + i, FLIGHT)

    def mate(i):
        other = lax.rem(me + lax.div(i, 2), FLIGHT)
        other_core = lax.rem(core + i, 2)
        return other, other_core, {"ctx": z * 2 + other_core, "exp": other}

    barrier = pltpu.get_barrier_semaphore()
    for other in (up, down, cross):
        pl.semaphore_signal(barrier, inc=1, device_id={"ctx": other}, device_id_type=MESH)

    def greet(i, carry):
        pl.semaphore_signal(barrier, inc=1, device_id=mate(i)[2], device_id_type=MESH)
        return carry

    lax.fori_loop(1, PLANE, greet, 0)
    loads = [
        pltpu.make_async_copy(src, dst, r.load_sem.at[i])
        for i, (src, dst) in enumerate(
            (
                (r.gate_in, r.gate),
                (r.out_w, r.w),
                (r.residual_in, r.residual),
                (r.router_in, r.router),
                (r.wi, r.ups.at[0]),
                (r.wo, r.downs.at[0]),
            )
        )
    ]
    for copy in loads:
        copy.start()

    raw = r.step[...]
    steps = jnp.maximum(raw, 0.0) + jnp.log1p(jnp.exp(-jnp.abs(raw)))
    r.steps[...] = steps
    rate = steps * (-jnp.exp(diagonal(r.decay[...])))
    pl.semaphore_wait(barrier, PLANE + 2)

    halos = [
        remote(
            r.x.at[pl.ds(COUNT - EDGE, EDGE)],
            r.halo_x,
            r.halo_send.at[0],
            r.halo_recv.at[0],
            {"ctx": after},
        ),
        remote(
            r.cpl.at[pl.ds(COUNT - EDGE, EDGE)],
            r.halo_c,
            r.halo_send.at[1],
            r.halo_recv.at[1],
            {"ctx": after},
        ),
    ]

    def hop(slot, src, dst, toward):
        return remote(src, dst, r.hop_send.at[slot], r.hop_recv.at[slot], {"ctx": toward})

    cut = SLICE // 2
    low_rows, high_rows = pl.ds(0, cut), pl.ds(cut, cut)
    up_early = hop(0, r.wi.at[low_rows], r.ups.at[1, low_rows], up)
    up_late = hop(1, r.wi.at[high_rows], r.ups.at[1, high_rows], up)
    ups_up = [None]
    ups_down = [hop(2, r.wi, r.ups.at[4], down)]
    downs_up = [hop(3, r.wo, r.downs.at[1], up)]
    downs_down = [hop(4, r.wo, r.downs.at[4], down)]
    for n in (1, 2):
        base = 4 * n + 1
        ups_up.append(hop(base, r.ups.at[n], r.ups.at[n + 1], up))
        ups_down.append(hop(base + 1, r.ups.at[n + 3], r.ups.at[n + 4], down))
        downs_up.append(hop(base + 2, r.downs.at[n], r.downs.at[n + 1], up))
        downs_down.append(hop(base + 3, r.downs.at[n + 3], r.downs.at[n + 4], down))
    ups_up.append(hop(13, r.ups.at[3, low_rows], r.ups.at[7, low_rows], up))
    ups_down.append(hop(14, r.ups.at[6, high_rows], r.ups.at[7, high_rows], down))
    downs_up.append(hop(15, r.downs.at[3, low_rows], r.downs.at[7, low_rows], up))
    downs_down.append(hop(16, r.downs.at[6, high_rows], r.downs.at[7, high_rows], down))

    @pl.when(c < 2 * RING - 1)
    def _():
        for copy in halos:
            copy.start()

    hold = (core == 1) & (z < RING - 1)
    up_early.start()
    ups_down[0].start()
    downs_down[0].start()

    @pl.when(jnp.logical_not(hold) | (z >= 4))
    def _():
        up_late.start()

    @pl.when(jnp.logical_not(hold))
    def _():
        downs_up[0].start()

    row = lax.broadcasted_iota(jnp.int32, (SPAN, SPAN), 0)
    col = lax.broadcasted_iota(jnp.int32, (SPAN, SPAN), 1)
    upper = (row <= col).astype(F32)
    above = row >= col
    expand = expander()
    for b in range(COUNT // SPAN):
        part = slice(b * SPAN, (b + 1) * SPAN)
        r.cums[:, part] = jnp.dot(
            rate[:, part], upper, precision=HIGH, preferred_element_type=F32
        )

    @pl.when(c > 0)
    def _():
        for copy in halos:
            copy.wait_recv()

    @pl.when(c == 0)
    def _():
        r.halo_x[...] = jnp.zeros_like(r.halo_x)
        r.halo_c[...] = jnp.zeros_like(r.halo_c)

    r.inner[...] = conv_part(r.x, r.halo_x[...].astype(F32), r.conv, r.pad)
    r.coup[...] = conv_part(r.cpl, r.halo_c[...].astype(F32), r.conv_cpl, r.pad_c)
    states = []
    drops = []
    for b in range(COUNT // SPAN):
        part = slice(b * SPAN, (b + 1) * SPAN)
        cums = r.cums[:, part]
        last = cums[:, SPAN - 1 : SPAN]
        tail = jnp.exp(last - cums) * r.steps[:, part]
        weighted = (r.inner[part, :].astype(F32) * spread_cols(tail, expand)).astype(BF16)
        states.append(
            lax.dot_general(
                r.coup[part, :STATE],
                weighted,
                (((0,), (0,)), ((), ())),
                preferred_element_type=F32,
            )
        )
        drops.append(spread_row(jnp.exp(last), expand))
    r.first[...] = states[0]
    run = drops[1] * states[0] + states[1]
    r.run[...] = run
    r.reach[...] = drops[0] * drops[1]
    r.drop[...] = drops[0]
    r.mine[...] = run.astype(BF16)

    def local_part():
        lane = lax.broadcasted_iota(jnp.int32, (SPAN, 2 * HDIM), 1)
        skip = spread_row(diagonal(r.skip[...]), expand)
        for b in range(COUNT // SPAN):
            part = slice(b * SPAN, (b + 1) * SPAN)
            scores = lax.dot_general(
                r.coup[part, STATE:],
                r.coup[part, :STATE],
                (((1,), (1,)), ((), ())),
                preferred_element_type=F32,
            )
            scores = jnp.where(above, scores, 0.0)
            cums = r.cums[:, part]
            turned = cums.T
            opened = silu(r.gate[part, :].astype(F32))
            r.growth[part, :] = spread_cols(jnp.exp(cums), expand) * opened
            for pair in range(HEADS // 2):
                cols = slice(pair * 2 * HDIM, (pair + 1) * 2 * HDIM)
                values = r.inner[part, cols]
                halves = []
                for h in (2 * pair, 2 * pair + 1):
                    spread = turned[:, h : h + 1] - cums[h : h + 1, :]
                    decay = jnp.exp(jnp.where(above, spread, 0.0))
                    mixing = (scores * decay * r.steps[h : h + 1, part]).astype(BF16)
                    halves.append(jnp.dot(mixing, values, preferred_element_type=F32))
                local = jnp.where(lane < HDIM, halves[0], halves[1])
                mixed = local + skip[:, cols] * values.astype(F32)
                r.gated[part, cols] = mixed * opened[:, cols]

    pairs = [
        remote(r.mine, r.theirs, r.pair_send.at[0], r.pair_recv.at[0], {"ctx": partner}),
        remote(r.reach, r.their_reach, r.pair_send.at[1], r.pair_recv.at[1], {"ctx": partner}),
    ]
    lines = STATE // CHUNKS
    spans = [pl.ds(i * lines, lines) for i in range(CHUNKS)]
    ahead = [
        remote(r.onward.at[s], r.arriving.at[s], r.chain_send.at[i], r.chain_recv.at[i], {"ctx": up})
        for i, s in enumerate(spans)
    ]
    relays = [
        remote(
            r.arriving.at[s],
            r.arriving.at[s],
            r.relay_send.at[i],
            r.chain_recv.at[i],
            {"ctx": partner},
        )
        for i, s in enumerate(spans)
    ]

    @pl.when(core == 0)
    def _():
        for copy in pairs:
            copy.start()

    loads[0].wait()
    early = z >= 3

    @pl.when(early)
    def _():
        local_part()

    @pl.when((core == 0) & (z == 0))
    def _():
        r.entry[...] = jnp.zeros_like(r.entry)

    @pl.when((core == 0) & (z > 0))
    def _():
        for i, s in enumerate(spans):
            relays[i].wait_recv()
            r.entry[s, :] = r.arriving[s, :].astype(F32)

    @pl.when(core == 1)
    def _():
        for copy in pairs:
            copy.wait_recv()

        @pl.when(z == 0)
        def _():
            for i, s in enumerate(spans):
                start = r.theirs[s, :].astype(F32)
                r.onward[s, :] = (r.reach[...] * start + r.run[s, :]).astype(BF16)
                ahead[i].start()
                r.entry[s, :] = start

        @pl.when(z > 0)
        def _():
            for i, s in enumerate(spans):
                start = r.theirs[s, :].astype(F32)
                ahead[i].wait_recv()
                inside = r.their_reach[...] * r.arriving[s, :].astype(F32) + start
                r.onward[s, :] = (r.reach[...] * inside + r.run[s, :]).astype(BF16)

                @pl.when(z < RING - 1)
                def _():
                    ahead[i].start()

                relays[i].start()
                r.entry[s, :] = inside

    @pl.when(hold & (z < 4))
    def _():
        up_late.start()

    @pl.when(hold)
    def _():
        downs_up[0].start()

    @pl.when(jnp.logical_not(early))
    def _():
        local_part()

    for b in range(COUNT // SPAN):
        part = slice(b * SPAN, (b + 1) * SPAN)
        entry = r.entry[...]
        if b == 1:
            entry = r.drop[...] * entry + r.first[...]
        carried = jnp.dot(r.coup[part, STATE:], entry.astype(BF16), preferred_element_type=F32)
        gated = r.gated[part, :] + carried * r.growth[part, :]
        r.gated[part, :] = gated
        scaled = (gated * r.norm_gain[...]).astype(BF16)
        r.byx[part, :] = scaled
        for k in range(SPAN // TOK):
            at_x, at_y = divmod(b * (SPAN // TOK) + k, 4)
            r.byy[(at_y * 4 + at_x) * TOK : (at_y * 4 + at_x + 1) * TOK, :] = scaled[
                k * TOK : (k + 1) * TOK, :
            ]

    half = D // 2
    quarter = half // 2
    low = pl.ds(0, quarter)
    high = pl.ds(quarter, quarter)

    def squares_copy(i):
        return remote(
            r.squares, r.all_squares.at[i], r.sq_send.at[i], r.sq_recv.at[i], {"exp": peer(i)}
        )

    def along_x(by):
        return {"exp": lax.rem(x + by, 4) * 4 + y}

    def along_y(by):
        return {"exp": x * 4 + lax.rem(y + by, 4)}

    def message(stage, side, number, src):
        slot = stage * 12 + side * 6 + number
        toward = along_x if side == stage else along_y
        landing = (r.near if stage == 0 else r.far).at[side, number]
        return remote(
            src,
            landing,
            r.ring_send.at[slot],
            r.ring_recv.at[slot],
            toward(1 if number % 2 == 0 else 3),
        )

    def block(stage, side, offset):
        if stage == 0:
            return r.parts.at[side, offset]
        place = y if side == 0 else x
        start = pl.multiple_of(lax.rem(place + offset, 4) * TOK, TOK)
        return r.joined.at[side, pl.ds(start, TOK)]

    def sources(stage, side):
        across = block(stage, side, 2)
        right = block(stage, side, 1)
        left = block(stage, side, 3)
        sums = r.near_sum if stage == 0 else r.far_sum
        return [
            across.at[:, low],
            across.at[:, high],
            right.at[:, high],
            left.at[:, low],
            sums.at[side, 0],
            sums.at[side, 1],
        ]

    copies = [
        [
            [message(stage, side, n, src) for n, src in enumerate(sources(stage, side))]
            for side in range(2)
        ]
        for stage in range(2)
    ]

    def multiply(side, offset):
        rows_ref = r.byx if side == 0 else r.byy
        place = x if side == 0 else y
        start = pl.multiple_of(lax.rem(place + offset, 4) * 128, 128)
        rows = rows_ref[pl.ds(start, 128), :]

        def one(i, carry):
            source = pl.ds(pl.multiple_of(side * half + i * 512, 512), 512)
            target = pl.ds(pl.multiple_of(i * 512, 512), 512)
            r.parts[side, offset, :, target] = jnp.dot(
                rows, r.w[:, source], preferred_element_type=F32
            ).astype(BF16)
            return carry

        lax.fori_loop(0, half // 512, one, 0)

    def pass_on(stage, side):
        landing = r.near if stage == 0 else r.far
        sums = r.near_sum if stage == 0 else r.far_sum
        copies[stage][side][0].wait_recv()
        sums[side, 0] = (
            block(stage, side, 1)[:, low].astype(F32) + landing[side, 0].astype(F32)
        ).astype(BF16)
        copies[stage][side][4].start()
        copies[stage][side][1].wait_recv()
        sums[side, 1] = (
            block(stage, side, 3)[:, high].astype(F32) + landing[side, 1].astype(F32)
        ).astype(BF16)
        copies[stage][side][5].start()

    def collect(stage, side):
        landing = r.near if stage == 0 else r.far
        for n in (2, 3, 4, 5):
            copies[stage][side][n].wait_recv()
        own = block(stage, side, 0)
        first = own[:, low].astype(F32) + landing[side, 4].astype(F32)
        first = first + landing[side, 3].astype(F32)
        second = own[:, high].astype(F32) + landing[side, 2].astype(F32)
        second = second + landing[side, 5].astype(F32)
        return first, second

    loads[1].wait()
    for side in range(2):
        multiply(side, 2)
        copies[0][side][0].start()
        copies[0][side][1].start()
    for side in range(2):
        multiply(side, 1)
        copies[0][side][2].start()
        multiply(side, 3)
        copies[0][side][3].start()
    up_early.wait_recv()
    up_late.wait_recv()
    ups_up[1].start()
    ups_down[0].wait_recv()
    ups_down[1].start()
    for side in range(2):
        pass_on(0, side)
    for side in range(2):
        multiply(side, 0)
    gated = r.gated[...]
    r.squares[...] = lax.dot_general(
        jnp.ones((8, WIDTH), F32),
        gated * gated,
        (((1,), (1,)), ((), ())),
        precision=HIGH,
        preferred_element_type=F32,
    )[0:1, :]

    def send_squares(i, carry):
        squares_copy(i).start()
        return carry

    lax.fori_loop(1, FLIGHT, send_squares, 0)
    downs_up[0].wait_recv()
    downs_up[1].start()
    downs_down[0].wait_recv()
    downs_down[1].start()
    for side in range(2):
        first, second = collect(0, side)
        r.joined[side, :, low] = first.astype(BF16)
        r.joined[side, :, high] = second.astype(BF16)
        for n in range(4):
            copies[1][side][n].start()
    for side in range(2):
        pass_on(1, side)
    for side in range(2):
        first, second = collect(1, side)
        r.owned[:, pl.ds(side * half, quarter)] = first
        r.owned[:, pl.ds(side * half + quarter, quarter)] = second
    r.all_squares[0] = r.squares[...]

    def take_squares(i, carry):
        squares_copy(i).wait()
        return carry

    lax.fori_loop(1, FLIGHT, take_squares, 0)
    total = r.all_squares[0]
    for i in range(1, FLIGHT):
        total = total + r.all_squares[i]

    loads[2].wait()
    loads[3].wait()
    wide_row = lax.broadcasted_iota(jnp.int32, (TOK, COUNT), 0)
    wide_col = lax.broadcasted_iota(jnp.int32, (TOK, COUNT), 1)
    squares = jnp.sum(
        jnp.where(wide_col == me * TOK + wide_row, total, 0.0), axis=1, keepdims=True
    )
    hidden = r.residual[...].astype(F32) + r.owned[...] * lax.rsqrt(squares / INNER + EPS)
    r.hidden[...] = hidden
    mean = jnp.sum(hidden * hidden, axis=1, keepdims=True) / D
    normed = (hidden * lax.rsqrt(mean + EPS) * r.moe_gain[...]).astype(BF16)
    for s in range(2 * RING):
        r.normed[s] = normed[:, s * SLICE : (s + 1) * SLICE]
    expert = lax.broadcasted_iota(jnp.int32, (TOK, NEXP), 1)
    named = expert < 0
    for k in range(TOPK):
        choice = diagonal(r.routes[k : k + 1, :].astype(F32))
        named = named | (choice.astype(jnp.int32) == expert)
    order = r.priority[...].astype(F32)
    earlier = (order < diagonal(order)).astype(F32).astype(BF16)
    rank = jnp.dot(earlier, named.astype(F32).astype(BF16), preferred_element_type=F32)
    key = jnp.where(named, rank, 99.0).astype(BF16)
    lanes = FLIGHT * CAP
    widen_row = lax.broadcasted_iota(jnp.int32, (NEXP, lanes), 0)
    widen_col = lax.broadcasted_iota(jnp.int32, (NEXP, lanes), 1)
    widen = (lax.div(widen_col, CAP) == widen_row).astype(F32).astype(BF16)
    key_wide = jnp.dot(key, widen, preferred_element_type=F32)
    slot = lax.rem(lax.broadcasted_iota(jnp.int32, (TOK, lanes), 1), CAP).astype(F32)
    chosen = (key_wide == slot).astype(F32)
    pick = chosen.astype(BF16)

    def source(n):
        if n <= 3:
            return lax.rem(z + RING - n, RING)
        if n <= 6:
            return lax.rem(z + n - 3, RING)
        return lax.rem(z + 4, RING)

    def row_copy(g, i):
        other, other_core, device = mate(i)
        return remote(
            r.rows.at[g, other_core, other],
            r.landed.at[g, me, core],
            r.row_send.at[g, i],
            r.row_recv.at[g, i],
            device,
        )

    own_rows = []
    for g in range(2):
        for j in range(2):
            for k, n in enumerate(GROUPS[g]):
                taken = lax.dot_general(
                    pick,
                    r.normed[2 * source(n) + j],
                    (((0,), (0,)), ((), ())),
                    preferred_element_type=F32,
                )
                r.rows[g, j, :, :, k * SLICE : (k + 1) * SLICE] = taken.reshape(
                    FLIGHT, CAP, SLICE
                ).astype(BF16)

        def start_rows(i, carry):
            row_copy(g, i).start()
            return carry

        lax.fori_loop(1, PLANE, start_rows, 0)
        own_rows.append(
            pltpu.make_async_copy(
                r.rows.at[g, core, me], r.landed.at[g, me, core], r.own_sem.at[g]
            )
        )
        own_rows[g].start()

    ups_up[1].wait_recv()
    ups_up[2].start()
    ups_down[1].wait_recv()
    ups_down[2].start()
    logits = lax.dot_general(
        normed, r.router[...], (((1,), (1,)), ((), ())), preferred_element_type=F32
    )
    raised = jnp.where(named, jnp.exp(logits), 0.0)
    share = (raised / jnp.sum(raised, axis=1, keepdims=True)).astype(BF16)
    share_wide = jnp.dot(share, widen, preferred_element_type=F32)
    r.share[...] = (chosen * share_wide).astype(BF16)
    downs_up[1].wait_recv()
    downs_up[2].start()
    downs_down[1].wait_recv()
    downs_down[2].start()

    loads[4].wait()
    loads[5].wait()
    for g in range(2):
        if g == 1:
            ups_up[2].wait_recv()
            ups_up[3].start()
            ups_down[2].wait_recv()
            ups_down[3].start()
        own_rows[g].wait()

        def take_rows(i, carry):
            row_copy(g, i).wait()
            return carry

        lax.fori_loop(1, PLANE, take_rows, 0)
        for k, n in enumerate(GROUPS[g]):
            cols = slice(k * SLICE, (k + 1) * SLICE)
            r.tokens[n] = (
                r.landed[g, :, :, :, cols].astype(F32).reshape(PLANE * CAP, SLICE).astype(BF16)
            )

        def gate_up(i, carry):
            cols = pl.ds(pl.multiple_of(i * 256, 256), 256)
            total = None if g == 0 else r.units[:, cols]
            for n in GROUPS[g]:
                if n == 7:
                    continue
                value = jnp.dot(r.tokens[n], r.ups[n, :, cols], preferred_element_type=F32)
                total = value if total is None else total + value
            r.units[:, cols] = total
            return carry

        lax.fori_loop(0, 2 * FFE // 256, gate_up, 0)
    downs_up[2].wait_recv()
    downs_up[3].start()
    downs_down[2].wait_recv()
    downs_down[3].start()
    ups_up[3].wait_recv()
    ups_down[3].wait_recv()

    def last_slice(i, carry):
        cols = pl.ds(pl.multiple_of(i * 256, 256), 256)
        total = r.units[:, cols] + jnp.dot(
            r.tokens[7], r.ups[7, :, cols], preferred_element_type=F32
        )
        r.units[:, cols] = total
        r.units_out[:, cols] = total.astype(BF16)
        return carry

    lax.fori_loop(0, 2 * FFE // 256, last_slice, 0)
    swap = remote(r.units_out, r.units_in, r.pair_send.at[2], r.pair_recv.at[2], {"ctx": partner})
    swap.start()
    swap.wait()
    gate = r.units[:, :FFE] + r.units_in[:, :FFE].astype(F32)
    lift = r.units[:, FFE:] + r.units_in[:, FFE:].astype(F32)
    activated = (silu(gate) * lift).astype(BF16)

    def back_copy(g, i):
        other, other_core, device = mate(i)
        return remote(
            r.answers.at[g, other, other_core],
            r.back.at[g, me, core],
            r.back_send.at[g, i],
            r.back_recv.at[g, i],
            device,
        )

    own_back = []
    for g in range(2):
        for k, n in enumerate(GROUPS[g]):
            if n == 7:
                downs_up[3].wait_recv()
                downs_down[3].wait_recv()
            values = lax.dot_general(
                activated, r.downs[n], (((1,), (1,)), ((), ())), preferred_element_type=F32
            )
            r.answers[g, :, :, :, k * SLICE : (k + 1) * SLICE] = values.reshape(
                FLIGHT, 2, CAP, SLICE
            ).astype(BF16)

        def start_back(i, carry):
            back_copy(g, i).start()
            return carry

        lax.fori_loop(1, PLANE, start_back, 0)
        own_back.append(
            pltpu.make_async_copy(
                r.answers.at[g, me, core], r.back.at[g, me, core], r.own_sem.at[2 + g]
            )
        )
        own_back[g].start()

    for g in range(2):
        own_back[g].wait()

        def take_back(i, carry):
            back_copy(g, i).wait()
            return carry

        lax.fori_loop(1, PLANE, take_back, 0)
        weights = r.share[...]
        for j in range(2):
            rows = r.back[g, :, j].astype(F32).reshape(FLIGHT * CAP, quarter).astype(BF16)
            total = jnp.dot(weights, rows, preferred_element_type=F32)
            for k, n in enumerate(GROUPS[g]):
                place = pl.multiple_of((2 * source(n) + j) * SLICE, SLICE)
                r.moe_out[:, pl.ds(place, SLICE)] = total[:, k * SLICE : (k + 1) * SLICE]

    @pl.when(c < 2 * RING - 1)
    def _():
        for copy in halos:
            copy.wait_send()

    @pl.when(core == 0)
    def _():
        for copy in pairs:
            copy.wait_send()

    @pl.when(hold)
    def _():
        for copy in ahead:
            copy.wait_send()

    @pl.when((core == 1) & (z > 0))
    def _():
        for copy in relays:
            copy.wait_send()

    for stage in range(2):
        for side in range(2):
            for copy in copies[stage][side]:
                copy.wait_send()
    for copy in [up_early, up_late] + ups_up[1:] + ups_down + downs_up + downs_down:
        copy.wait_send()


def body(
    inner_input,
    gate_input,
    coupling_input,
    step_input,
    conv_inner,
    conv_coupling,
    decay_log,
    skip_gain,
    norm_gain,
    out_weight,
    residual,
    moe_gain,
    router_weight,
    routes,
    priority,
    expert_in,
    expert_out,
):
    return pl.pallas_call(
        layer_kernel,
        out_shape=(shaped((TOK, D), F32), shaped((TOK, D), F32)),
        in_specs=[vmem()] * 11 + [anyspace()] * 6,
        out_specs=(vmem(), vmem()),
        scratch_shapes=list(scratch().values()),
        compiler_params=pltpu.CompilerParams(
            vmem_limit_bytes=VMEM_LIMIT, collective_id=0, has_side_effects=True
        ),
    )(
        inner_input,
        coupling_input,
        step_input.T,
        conv_inner,
        conv_coupling,
        decay_log[None, :],
        skip_gain[None, :],
        norm_gain[None, :],
        moe_gain[None, :],
        routes.T,
        priority,
        gate_input,
        out_weight,
        residual,
        router_weight.T,
        expert_in[0],
        expert_out[0],
    )


def solution(mesh):
    placed = (
        P("ctx", "exp"),
        P("ctx", "exp"),
        P("ctx", None),
        P("ctx", "exp"),
        P(None, "exp"),
        P(),
        P("exp"),
        P("exp"),
        P("exp"),
        P("exp", None),
        P(("ctx", "exp"), None),
        P(),
        P(),
        P(("ctx", "exp"), None),
        P(("ctx", "exp"), None),
        P("exp", "ctx", None),
        P("exp", "ctx", None),
    )
    return jax.shard_map(
        body,
        mesh=mesh,
        in_specs=placed,
        out_specs=(P(("ctx", "exp"), None), P(("ctx", "exp"), None)),
        check_vma=False,
    )
```

time: 356 us -> 135 us (0.38)
  waiting for transfers between devices: 209 us -> 0 us
  Pallas kernels: 0 us -> 130 us
  blocking collectives: 69.2 us -> 0 us
  matrix products: 25 us -> 0 us
  between operations: 14.8 us -> 0.65 us
  other arithmetic: 13 us -> 0 us
  starting transfers between devices: 11.6 us -> 0 us
  local copies, waits for them, and re-layouts: 11.2 us -> 3.74 us
    pallas_call x0 -> x1, Pallas kernels: none -> 130 us  [body(): pl.pallas_call(layer_kernel, out_shape=(shaped((TOK, D), F32), shaped((TO...]
    all_gather x3 -> x0, waiting for transfers between devices: 121 us -> none  [the longest x1 59.4 us: body(): whole_in = lax.all_gather(expert_in[0], 'ctx', axis=0, tiled=True)]
    reduce_scatter x1 -> x0, waiting for transfers between devices: 70.9 us -> none  [body(): lax.psum_scatter(projected.astype(jnp.bfloat16), 'exp', scatter_dimension...]
    unnamed x1 -> x0, blocking collectives: 32.9 us -> none
    dot_general x9 -> x0, matrix products: 23.5 us -> none  [the longest x1 6.61 us: body(): jnp.einsum('rkw,kwf->krf', rows.reshape(rows.shape[0], slices, slice_widt...]
    all_gather x1 -> x0, blocking collectives: 18.8 us -> none  [carried_in(): gathered = jax.tree.map(lambda a: lax.all_gather(a, axis), part)]
    all_to_all x1 -> x0, blocking collectives: 17.5 us -> none  [body(): lax.all_to_all(outbound, 'exp', split_axis=0, concat_axis=0, tiled=True)]
    all_to_all x1 -> x0, waiting for transfers between devices: 15.2 us -> none  [body(): lax.all_to_all(answer.reshape(flight, capacity, answer.shape[1]), 'exp',...]
  transfers between devices with their start and end apart: 6 -> 0, of which waited for: 5 -> 0; matrix products, arithmetic and copies ran while one was open for 6% -> 0% of each run, Pallas kernels for 0% -> 0%
where the time goes in v2:
time: 135 us
  Pallas kernels  130 us (96%)
  local copies, waits for them, and re-layouts  3.74 us (3%)
    pallas_call x1, Pallas kernels, body(): pl.pallas_call(layer_kernel, out_shape=(shaped((TOK, D), F32), shaped((TO...  130 us
    unnamed x2, local copies, waits for them, and re-layouts  3.74 us

profile of v2, /device:TPU:1, one launch (start us, length us, event | category | flops | bytes accessed | tf_op | source)
XLA Modules:
  0.0 134.5 jit_solution(11796489388672862004)
XLA Ops:
  0.6 130.2 %shard_map.176 = (f32[32,4096]{1,0:T(8,128)}, f32[32,4096]{1,0:T(8,128)}) custom-call(bf16[512,512]{1,0:T(8,128)(2,1)} %refs_0_.1, bf16[512,256]{1,0:T(8,128)(2,1)} %refs_1_.1, f32[8,512]{1,0:T(8,128)} %bitcast.12, f32[4,512]{1,0:T(4,128)} %refs_3_.1, f32[4,256]{1,0:T(4,128)} %refs_4_.1, f32[1,8]{1,0:T(1,128)} %bitcast.16, f32[1,8]{1,0:T(1,128)} %bitcast.17, ...), custom_call_target="tpu_custom_call" | custom-call | tf_op jit(solution)/shard_map/pallas_call | solution.py:895
  130.8 1.9 %copy.21 = f32[32,4096]{1,0:T(8,128)} copy(f32[32,4096]{1,0:T(8,128)} %get-tuple-element.4) | data formatting | bytes 1048576
  132.7 1.9 %copy.22 = f32[32,4096]{1,0:T(8,128)} copy(f32[32,4096]{1,0:T(8,128)} %get-tuple-element.5) | data formatting | bytes 1048576

commit v3 on v2

--- a/solution.py
+++ b/solution.py
@@ -473,6 +473,9 @@
     def _():
         local_part()
 
+    ups_down[0].wait_recv()
+    ups_down[1].start()
+
     for b in range(COUNT // SPAN):
         part = slice(b * SPAN, (b + 1) * SPAN)
         entry = r.entry[...]
@@ -592,18 +595,20 @@
         multiply(side, 2)
         copies[0][side][0].start()
         copies[0][side][1].start()
+    up_early.wait_recv()
+    up_late.wait_recv()
+    ups_up[1].start()
     for side in range(2):
         multiply(side, 1)
         copies[0][side][2].start()
         multiply(side, 3)
         copies[0][side][3].start()
-    up_early.wait_recv()
-    up_late.wait_recv()
-    ups_up[1].start()
-    ups_down[0].wait_recv()
-    ups_down[1].start()
+    downs_down[0].wait_recv()
+    downs_down[1].start()
     for side in range(2):
         pass_on(0, side)
+    downs_up[0].wait_recv()
+    downs_up[1].start()
     for side in range(2):
         multiply(side, 0)
     gated = r.gated[...]
@@ -620,18 +625,22 @@
         return carry
 
     lax.fori_loop(1, FLIGHT, send_squares, 0)
-    downs_up[0].wait_recv()
-    downs_up[1].start()
-    downs_down[0].wait_recv()
-    downs_down[1].start()
     for side in range(2):
         first, second = collect(0, side)
         r.joined[side, :, low] = first.astype(BF16)
         r.joined[side, :, high] = second.astype(BF16)
         for n in range(4):
             copies[1][side][n].start()
+    ups_down[1].wait_recv()
+    ups_down[2].start()
+    ups_up[1].wait_recv()
+    ups_up[2].start()
     for side in range(2):
         pass_on(1, side)
+    downs_down[1].wait_recv()
+    downs_down[2].start()
+    downs_up[1].wait_recv()
+    downs_up[2].start()
     for side in range(2):
         first, second = collect(1, side)
         r.owned[:, pl.ds(side * half, quarter)] = first
@@ -721,10 +730,6 @@
         )
         own_rows[g].start()
 
-    ups_up[1].wait_recv()
-    ups_up[2].start()
-    ups_down[1].wait_recv()
-    ups_down[2].start()
     logits = lax.dot_general(
         normed, r.router[...], (((1,), (1,)), ((), ())), preferred_element_type=F32
     )
@@ -732,19 +737,19 @@
     share = (raised / jnp.sum(raised, axis=1, keepdims=True)).astype(BF16)
     share_wide = jnp.dot(share, widen, preferred_element_type=F32)
     r.share[...] = (chosen * share_wide).astype(BF16)
-    downs_up[1].wait_recv()
-    downs_up[2].start()
-    downs_down[1].wait_recv()
-    downs_down[2].start()
+    ups_down[2].wait_recv()
+    ups_down[3].start()
+    ups_up[2].wait_recv()
+    ups_up[3].start()
 
     loads[4].wait()
     loads[5].wait()
     for g in range(2):
         if g == 1:
-            ups_up[2].wait_recv()
-            ups_up[3].start()
-            ups_down[2].wait_recv()
-            ups_down[3].start()
+            downs_up[2].wait_recv()
+            downs_up[3].start()
+            downs_down[2].wait_recv()
+            downs_down[3].start()
         own_rows[g].wait()
 
         def take_rows(i, carry):
@@ -770,10 +775,6 @@
             return carry
 
         lax.fori_loop(0, 2 * FFE // 256, gate_up, 0)
-    downs_up[2].wait_recv()
-    downs_up[3].start()
-    downs_down[2].wait_recv()
-    downs_down[3].start()
     ups_up[3].wait_recv()
     ups_down[3].wait_recv()
 

time: 135 us -> 131 us (0.970)
  Pallas kernels: 130 us -> 126 us
    pallas_call x1, Pallas kernels: 130 us -> 126 us  [body(): pl.pallas_call(layer_kernel, out_shape=(shaped((TOK, D), F32), shaped((TO...]
where the time goes in v3:
time: 131 us
  Pallas kernels  126 us (96%)
  local copies, waits for them, and re-layouts  3.74 us (3%)
    pallas_call x1, Pallas kernels, body(): pl.pallas_call(layer_kernel, out_shape=(shaped((TOK, D), F32), shaped((TO...  126 us
    unnamed x2, local copies, waits for them, and re-layouts  3.74 us

profile of v3, /device:TPU:1, one launch (start us, length us, event | category | flops | bytes accessed | tf_op | source)
XLA Modules:
  0.0 130.7 jit_solution(13632353490249680229)
XLA Ops:
  0.6 126.3 %shard_map.176 = (f32[32,4096]{1,0:T(8,128)}, f32[32,4096]{1,0:T(8,128)}) custom-call(bf16[512,512]{1,0:T(8,128)(2,1)} %refs_0_.1, bf16[512,256]{1,0:T(8,128)(2,1)} %refs_1_.1, f32[8,512]{1,0:T(8,128)} %bitcast.12, f32[4,512]{1,0:T(4,128)} %refs_3_.1, f32[4,256]{1,0:T(4,128)} %refs_4_.1, f32[1,8]{1,0:T(1,128)} %bitcast.16, f32[1,8]{1,0:T(1,128)} %bitcast.17, ...), custom_call_target="tpu_custom_call" | custom-call | tf_op jit(solution)/shard_map/pallas_call | solution.py:896
  127.0 1.9 %copy.21 = f32[32,4096]{1,0:T(8,128)} copy(f32[32,4096]{1,0:T(8,128)} %get-tuple-element.4) | data formatting | bytes 1048576
  128.8 1.9 %copy.22 = f32[32,4096]{1,0:T(8,128)} copy(f32[32,4096]{1,0:T(8,128)} %get-tuple-element.5) | data formatting | bytes 1048576

commit v4 on v3

--- a/solution.py
+++ b/solution.py
@@ -188,8 +188,8 @@
         "load_sem": dma((6,)),
         "halo_send": dma((2,)),
         "halo_recv": dma((2,)),
-        "pair_send": dma((3,)),
-        "pair_recv": dma((3,)),
+        "pair_send": dma((8,)),
+        "pair_recv": dma((8,)),
         "chain_send": dma((CHUNKS,)),
         "chain_recv": dma((CHUNKS,)),
         "relay_send": dma((CHUNKS,)),
@@ -778,22 +778,33 @@
     ups_up[3].wait_recv()
     ups_down[3].wait_recv()
 
-    def last_slice(i, carry):
-        cols = pl.ds(pl.multiple_of(i * 256, 256), 256)
+    swaps = []
+    blocks = [(pl.ds(i, 256), pl.ds(FFE + i, 256)) for i in range(0, FFE, 256)]
+    for cols in sum(blocks, ()):
         total = r.units[:, cols] + jnp.dot(
             r.tokens[7], r.ups[7, :, cols], preferred_element_type=F32
         )
         r.units[:, cols] = total
         r.units_out[:, cols] = total.astype(BF16)
-        return carry
-
-    lax.fori_loop(0, 2 * FFE // 256, last_slice, 0)
-    swap = remote(r.units_out, r.units_in, r.pair_send.at[2], r.pair_recv.at[2], {"ctx": partner})
-    swap.start()
-    swap.wait()
-    gate = r.units[:, :FFE] + r.units_in[:, :FFE].astype(F32)
-    lift = r.units[:, FFE:] + r.units_in[:, FFE:].astype(F32)
-    activated = (silu(gate) * lift).astype(BF16)
+        slot = 2 + len(swaps)
+        swaps.append(
+            remote(
+                r.units_out.at[:, cols],
+                r.units_in.at[:, cols],
+                r.pair_send.at[slot],
+                r.pair_recv.at[slot],
+                {"ctx": partner},
+            )
+        )
+        swaps[-1].start()
+    pieces = []
+    for i, (gate_cols, lift_cols) in enumerate(blocks):
+        swaps[2 * i].wait_recv()
+        gate = r.units[:, gate_cols] + r.units_in[:, gate_cols].astype(F32)
+        swaps[2 * i + 1].wait_recv()
+        lift = r.units[:, lift_cols] + r.units_in[:, lift_cols].astype(F32)
+        pieces.append((silu(gate) * lift).astype(BF16))
+    activated = jnp.concatenate(pieces, axis=1)
 
     def back_copy(g, i):
         other, other_core, device = mate(i)
@@ -870,7 +881,7 @@
         for side in range(2):
             for copy in copies[stage][side]:
                 copy.wait_send()
-    for copy in [up_early, up_late] + ups_up[1:] + ups_down + downs_up + downs_down:
+    for copy in swaps + [up_early, up_late] + ups_up[1:] + ups_down + downs_up + downs_down:
         copy.wait_send()
 
 

time: 131 us -> 130 us (level)
    pallas_call x1, Pallas kernels: 126 us -> 125 us  [body(): pl.pallas_call(layer_kernel, out_shape=(shaped((TOK, D), F32), shaped((TO...]
where the time goes in v4:
time: 130 us; the launch traced here: 129 us
  Pallas kernels  125 us (96%)
  local copies, waits for them, and re-layouts  3.74 us (3%)
    pallas_call x1, Pallas kernels, body(): pl.pallas_call(layer_kernel, out_shape=(shaped((TOK, D), F32), shaped((TO...  125 us
    unnamed x2, local copies, waits for them, and re-layouts  3.74 us

profile of v4, /device:TPU:1, one launch (start us, length us, event | category | flops | bytes accessed | tf_op | source)
XLA Modules:
  0.0 129.3 jit_solution(5444151338799799389)
XLA Ops:
  0.6 124.9 %shard_map.176 = (f32[32,4096]{1,0:T(8,128)}, f32[32,4096]{1,0:T(8,128)}) custom-call(bf16[512,512]{1,0:T(8,128)(2,1)} %refs_0_.1, bf16[512,256]{1,0:T(8,128)(2,1)} %refs_1_.1, f32[8,512]{1,0:T(8,128)} %bitcast.12, f32[4,512]{1,0:T(4,128)} %refs_3_.1, f32[4,256]{1,0:T(4,128)} %refs_4_.1, f32[1,8]{1,0:T(1,128)} %bitcast.16, f32[1,8]{1,0:T(1,128)} %bitcast.17, ...), custom_call_target="tpu_custom_call" | custom-call | tf_op jit(solution)/shard_map/pallas_call | solution.py:907
  125.6 1.9 %copy.21 = f32[32,4096]{1,0:T(8,128)} copy(f32[32,4096]{1,0:T(8,128)} %get-tuple-element.4) | data formatting | bytes 1048576
  127.5 1.9 %copy.22 = f32[32,4096]{1,0:T(8,128)} copy(f32[32,4096]{1,0:T(8,128)} %get-tuple-element.5) | data formatting | bytes 1048576
